TPU v7x, 256 devices: a whole 4x4x8 slice. The times are simulated.
256 devices in a mesh: shot: 32 (over z, x_hi, core), dom: 8 (over y, x_lo).
Axes of the slice: x: 4 (x_hi: 2, x_lo: 2; x = x_hi * 2 + x_lo), y: 4, z: 8, core: 2. Of those that a mesh axis runs over, the one named last changes fastest.
Arguments:
- velocity: float32 [64, 128, 256], P('dom', 'shot'), may hold values from 0.15 to 0.4
- epsilon: float32 [64, 128, 256], P('dom', 'shot'), may hold values from 0.05 to 0.3
- forward_state: float32 [32, 4, 64, 128, 256], P('shot', None, 'dom'), may hold values from -1.2 to 1.2
- adjoint_state: float32 [32, 4, 64, 128, 256], P('shot', None, 'dom'), may hold values from -1.2 to 1.2
- source_cell: int32 [32], P('shot'), may hold values from 0 to 2097151
- wavelet: float32 [32, 3], P('shot'), may hold values from -6 to 6
- receiver_cells: int32 [32, 256], P('shot'), may hold values from 0 to 2097151
- residuals: float32 [32, 4, 256], P('shot'), may hold values from -6 to 6
Outputs:
- velocity_grad: float32 [64, 128, 256], P('dom', 'shot')
- epsilon_grad: float32 [64, 128, 256], P('dom', 'shot')
Inputs may be any that keep to these rules, and one draw needn't show every extreme that they name: `source_cell`: flat grid cell index (z * 128 + x) * 256 + y of each shot's source. `receiver_cells`: flat grid cell indices (z * 128 + x) * 256 + y of each shot's receivers; two receivers may share a cell.
All inputs are finite; a program needn't handle non-finite values.
Results may differ from a plain program's by a relative error of at most 0.00002.
Values sent between devices are 32-bit elements; how exact they have to be, the bound alone decides.
No kernel may reach another device: no remote copies, remote signals or barrier semaphores. Data moves between devices by JAX's collectives and lax.ppermute only.
A program may use at most 128 MiB of HBM per device.

v0:
```python
import jax
import jax.numpy as jnp
from jax import lax
from jax.sharding import PartitionSpec as P

STEPS = 4


def with_halo(cells, sides, width):
    for axis, dim in sides:
        count = lax.axis_size(axis)
        ends = count - 1
        head = lax.slice_in_dim(cells, 0, width, axis=dim)
        tail = lax.slice_in_dim(cells, cells.shape[dim] - width, cells.shape[dim], axis=dim)
        cells = jnp.concatenate(
            [
                lax.ppermute(tail, axis, [(i, (i + 1) % count) for i in range(ends)]),
                cells,
                lax.ppermute(head, axis, [((i + 1) % count, i) for i in range(ends)]),
            ],
            axis=dim,
        )
    return cells


def stencil(padded, axis, size):

    def part(offset):
        return lax.slice_in_dim(padded, offset, offset + size, axis=axis)

    return 4.0 / 3.0 * (part(1) + part(3)) - 1.0 / 12.0 * (part(0) + part(4)) - 2.5 * part(2)


def second_diff(field, axis):
    widths = [(0, 0), (0, 0), (0, 0)]
    widths[axis] = (2, 2)
    return stencil(jnp.pad(field, widths), axis, field.shape[axis])


def lateral(field):
    return second_diff(field, 1) + second_diff(field, 2)


def forward_vertical(field):
    padded = with_halo(field, (("dom", 0),), 2)
    return stencil(padded, 0, field.shape[0])


def adjoint_vertical(field):
    padded = with_halo(field, (("dom", 0),), 2)
    return stencil(padded, 0, field.shape[0])


def sum_shots(first_term, second_term, share_rows):
    whole_one, whole_two = lax.psum((first_term, second_term), "shot")
    offset = lax.axis_index("shot") * share_rows
    return (
        lax.dynamic_slice_in_dim(whole_one, offset, share_rows, 1),
        lax.dynamic_slice_in_dim(whole_two, offset, share_rows, 1),
    )


def on_device(
    velocity, epsilon, forward_state, adjoint_state, source_cell, wavelet, receiver_cells, residuals
):
    vel_slab, eps_slab = (
        lax.all_gather(velocity, "shot", axis=1, tiled=True),
        lax.all_gather(epsilon, "shot", axis=1, tiled=True),
    )
    stiffness = vel_slab * vel_slab
    stretch = 1.0 + 2.0 * eps_slab
    slab_depth, slab_width, slab_length = stiffness.shape
    plane_size = slab_width * slab_length
    first_layer = lax.axis_index("dom") * slab_depth

    def inject(field, cell_ids, amounts):
        layer_ids = cell_ids // plane_size - first_layer
        inside = (layer_ids >= 0) & (layer_ids < slab_depth)
        layer_ids = jnp.where(inside, layer_ids, 0)
        within = cell_ids % plane_size
        flattened = (
            field.reshape(-1)
            .at[layer_ids * plane_size + within]
            .add(jnp.where(inside, amounts, 0.0))
        )
        return flattened.reshape(field.shape)

    source = source_cell[0]
    receivers = receiver_cells[0]
    pressure_old, pressure_now = (forward_state[0, 0], forward_state[0, 1])
    support_old, support_now = (forward_state[0, 2], forward_state[0, 3])
    flat_terms = []
    depth_terms = []
    for moment in range(STEPS):
        flat_term = lateral(pressure_now)
        depth_term = forward_vertical(support_now)
        flat_terms.append(flat_term)
        depth_terms.append(depth_term)
        if moment + 1 < STEPS:
            pressure_new = (
                2.0 * pressure_now - pressure_old + stiffness * (stretch * flat_term + depth_term)
            )
            support_new = 2.0 * support_now - support_old + stiffness * (flat_term + depth_term)
            pressure_new = inject(pressure_new, source, wavelet[0, moment])
            support_new = inject(support_new, source, wavelet[0, moment])
            pressure_old, pressure_now = (pressure_now, pressure_new)
            support_old, support_now = (support_now, support_new)
    back_old, back_now = (adjoint_state[0, 0], adjoint_state[0, 1])
    side_old, side_now = (adjoint_state[0, 2], adjoint_state[0, 3])
    image_one = jnp.zeros_like(stiffness)
    image_two = jnp.zeros_like(stiffness)
    for moment in reversed(range(STEPS)):
        back_new = 2.0 * back_now - back_old + lateral(stiffness * (stretch * back_now + side_now))
        back_new = inject(back_new, receivers, residuals[0, moment])
        side_new = 2.0 * side_now - side_old + adjoint_vertical(stiffness * (back_now + side_now))
        image_one = image_one + back_new * flat_terms[moment]
        image_two = (
            image_two
            + back_new * depth_terms[moment]
            + side_new * (flat_terms[moment] + depth_terms[moment])
        )
        back_old, back_now = (back_now, back_new)
        side_old, side_now = (side_now, side_new)
    share_rows = velocity.shape[1]
    vel_term = 2.0 * vel_slab * (stretch * image_one + image_two)
    eps_term = 2.0 * stiffness * image_one
    velocity_grad, epsilon_grad = sum_shots(vel_term, eps_term, share_rows)
    return (velocity_grad, epsilon_grad)


def solution(mesh):
    placed = (
        P("dom", "shot", None),
        P("dom", "shot", None),
        P("shot", None, "dom", None, None),
        P("shot", None, "dom", None, None),
        P("shot"),
        P("shot", None),
        P("shot", None),
        P("shot", None, None),
    )
    return jax.shard_map(
        on_device,
        mesh=mesh,
        in_specs=placed,
        out_specs=(P("dom", "shot", None), P("dom", "shot", None)),
        check_vma=False,
    )
```

profile of v0, /device:TPU:1, one launch (start us, length us, event | category | flops | bytes accessed | tf_op | source)
XLA Modules:
  0.0 653.4 jit_solution(7060213678199251076)
XLA Ops:
  20.1 7.6 %collective-permute-done.1 = f32[2,128,256]{2,1,0:T(8,128)S(1)} collective-permute-done((f32[2,128,256]{2,1,0:T(8,128)S(1)}, f32[2,128,256]{2,1,0:T(8,128)S(1)}, u32[]{:S(2)}, u32[]{:S(2)}) %collective-permute-start.1) | collective-permute-done | bytes 262176 | tf_op jit(solution)/shard_map/ppermute | solution.py:19
  27.7 65.5 %all-gather.3.cloned.1.call-done = f32[8,128,256]{2,0,1:T(8,128)} async-done(((f32[8,4,256]{2,0,1:T(8,128)}), f32[8,128,256]{2,0,1:T(8,128)}) %all-gather.3.cloned.1.call-update) | async-done | bytes 1048592 | tf_op jit(solution)/shard_map/all_gather | solution.py:67
  93.2 78.1 %all-gather.5.cloned.1.call-done = f32[8,128,256]{2,0,1:T(8,128)} async-done(((f32[8,4,256]{2,0,1:T(8,128)}), f32[8,128,256]{2,0,1:T(8,128)}) %all-gather.5.cloned.1.call-update) | async-done | bytes 1048592 | tf_op jit(solution)/shard_map/all_gather | solution.py:68
  171.3 5.2 fusion.121
  189.9 6.9 %collective-permute-done.3 = f32[2,128,256]{2,1,0:T(8,128)S(1)} collective-permute-done((f32[2,128,256]{2,1,0:T(8,128)}, f32[2,128,256]{2,1,0:T(8,128)S(1)}, u32[]{:S(2)}, u32[]{:S(2)}) %collective-permute-start.3) | collective-permute-done | bytes 262176 | tf_op jit(solution)/shard_map/ppermute | solution.py:19
  196.8 4.2 multiply_add_fusion.4
  208.1 4.9 collective-permute-start.4
  227.7 4.4 collective-permute-done.5
  242.7 5.0 fusion.123
  256.4 4.2 scatter_fusion
  262.4 5.0 add_multiply_fusion.5
  267.5 4.0 add_multiply_fusion.4
  273.4 4.5 collective-permute-start.8
  288.6 4.3 scatter_fusion.1
  296.1 4.9 add_multiply_fusion.2
  301.9 4.6 collective-permute-start.10
  311.8 4.1 scatter_fusion.2
  318.4 6.1 add_multiply_fusion.1
  327.2 4.3 scatter_fusion.3
  334.0 9.8 %multiply_multiply_fusion = (f32[8,128,256]{2,1,0:T(8,128)}, f32[8,128,256]{2,1,0:T(8,128)}, f32[8,128,256]{2,1,0:T(8,128)}) fusion(f32[8,128,256]{2,1,0:T(8,128)} %reshape.380, f32[8,128,256]{2,1,0:T(8,128)} %copy-done.13, f32[8,128,256]{2,1,0:T(8,128)} %reshape.378, f32[8,128,256]{2,1,0:T(8,128)} %copy-done.15, f32[8,128,256]{2,1,0:T(8,128)S(1)} %reshape.376, ...), kind=kLoop, calls=%fused_computation.209 | loop fusion | flops 6815744 | bytes 13631488 | tf_op jit(solution)/shard_map/mul | solution.py:126
  345.1 4.9 collective-permute-start.14
  353.7 5.5 collective-permute-done.15
  359.3 7.9 %fusion.9 = f32[8,128,256]{2,1,0:T(8,128)} fusion(f32[8,128,256]{2,1,0:T(8,128)} %get-tuple-element.104, f32[2,128,256]{2,1,0:T(8,128)S(1)} %collective-permute-done.15, f32[2,128,256]{2,1,0:T(8,128)S(1)} %collective-permute-done.14, f32[8,128,256]{2,1,0:T(8,128)S(1)} %copy-done.11, f32[8,128,256]{2,1,0:T(8,128)} %get-tuple-element.92, ...), kind=kLoop, calls=%fused_computation.65 | loop fusion | flops 13893632 | bytes 24641536 | tf_op jit(solution)/shard_map/mul | solution.py:125
  367.2 277.8 %all-reduce.19.cloned.1.call-done = (f32[8,128,256]{2,1,0:T(8,128)}, f32[8,128,256]{2,1,0:T(8,128)}) async-done(((f32[8,128,256]{2,1,0:T(8,128)}, f32[8,128,256]{2,1,0:T(8,128)}), (f32[8,128,256]{2,1,0:T(8,128)}, f32[8,128,256]{2,1,0:T(8,128)})) %all-reduce.19.cloned.1.call-update) | async-done | bytes 2097168 | tf_op jit(solution)/shard_map/psum | solution.py:55
  (165 shorter events, 102.3 us)
Async XLA Ops:
  7.2 86.1 %all-gather.3.cloned.1.call-start = ((), (), s32[]{:S(2)}) async-start(), calls=%async_computation | async-start | bytes 1081344 | tf_op jit(solution)/shard_map/all_gather | solution.py:67
  8.6 162.7 %all-gather.5.cloned.1.call-start = ((), (), s32[]{:S(2)}) async-start(), calls=%async_computation.1 | async-start | bytes 1081344 | tf_op jit(solution)/shard_map/all_gather | solution.py:68
  10.1 634.9 %all-reduce.19.cloned.1.call-start = ((), (), s32[]{:S(2)}) async-start(), calls=%async_computation.2 | async-start | bytes 4194304 | tf_op jit(solution)/shard_map/psum | solution.py:55
  11.2 8.9 %collective-permute-start = (f32[2,128,256]{2,1,0:T(8,128)S(1)}, f32[2,128,256]{2,1,0:T(8,128)S(1)}, u32[]{:S(2)}, u32[]{:S(2)}) collective-permute-start(f32[2,128,256]{2,1,0:T(8,128)S(1)} %get-tuple-element.99), channel_id=1, source_target_pairs={{0,1},{1,2},{2,3},{3,4},{4,5},{5,6},{6,7},{8,9},{9,10},{10,11},{11... | collective-permute-start | bytes 786440 | tf_op jit(solution)/shard_map/ppermute | solution.py:17
  15.2 12.6 %collective-permute-start.1 = (f32[2,128,256]{2,1,0:T(8,128)S(1)}, f32[2,128,256]{2,1,0:T(8,128)S(1)}, u32[]{:S(2)}, u32[]{:S(2)}) collective-permute-start(f32[2,128,256]{2,1,0:T(8,128)S(1)} %get-tuple-element.100), channel_id=1, source_target_pairs={{1,0},{2,1},{3,2},{4,3},{5,4},{6,5},{7,6},{9,8},{10,9},{11,10},{12... | collective-permute-start | bytes 786440 | tf_op jit(solution)/shard_map/ppermute | solution.py:19
  27.7 143.6 %copy-start.31 = (f32[2,128,256]{2,1,0:T(8,128)}, f32[2,128,256]{2,1,0:T(8,128)S(1)}, u32[]{:S(2)}) copy-start(f32[2,128,256]{2,1,0:T(8,128)S(1)} %collective-permute-done.1) | copy-start | bytes 786436
  179.5 9.2 %collective-permute-start.2 = (f32[2,128,256]{2,1,0:T(8,128)}, f32[2,128,256]{2,1,0:T(8,128)}, u32[]{:S(2)}, u32[]{:S(2)}) collective-permute-start(f32[2,128,256]{2,1,0:T(8,128)} %slice.602), channel_id=1, source_target_pairs={{0,1},{1,2},{2,3},{3,4},{4,5},{5,6},{6,7},{8,9},{9,10},{10,11},{11... | collective-permute-start | bytes 786440 | tf_op jit(solution)/shard_map/ppermute | solution.py:17
  187.4 9.4 %collective-permute-start.3 = (f32[2,128,256]{2,1,0:T(8,128)}, f32[2,128,256]{2,1,0:T(8,128)S(1)}, u32[]{:S(2)}, u32[]{:S(2)}) collective-permute-start(f32[2,128,256]{2,1,0:T(8,128)} %slice.605), channel_id=1, source_target_pairs={{1,0},{2,1},{3,2},{4,3},{5,4},{6,5},{7,6},{9,8},{10,9},{11,10},{12... | collective-permute-start | bytes 786440 | tf_op jit(solution)/shard_map/ppermute | solution.py:19
  208.1 17.1 %collective-permute-start.4 = (f32[2,128,256]{2,1,0:T(8,128)}, f32[2,128,256]{2,1,0:T(8,128)}, u32[]{:S(2)}, u32[]{:S(2)}) collective-permute-start(f32[2,128,256]{2,1,0:T(8,128)} %slice.619), channel_id=1, source_target_pairs={{0,1},{1,2},{2,3},{3,4},{4,5},{5,6},{6,7},{8,9},{9,10},{10,11},{11... | collective-permute-start | bytes 786440 | tf_op jit(solution)/shard_map/ppermute | solution.py:17
  223.9 8.2 %collective-permute-start.5 = (f32[2,128,256]{2,1,0:T(8,128)}, f32[2,128,256]{2,1,0:T(8,128)S(1)}, u32[]{:S(2)}, u32[]{:S(2)}) collective-permute-start(f32[2,128,256]{2,1,0:T(8,128)} %slice.622), channel_id=1, source_target_pairs={{1,0},{2,1},{3,2},{4,3},{5,4},{6,5},{7,6},{9,8},{10,9},{11,10},{12... | collective-permute-start | bytes 786440 | tf_op jit(solution)/shard_map/ppermute | solution.py:19
  239.2 55.2 %collective-permute-start.12 = (f32[2,128,256]{2,1,0:T(8,128)}, f32[2,128,256]{2,1,0:T(8,128)}, u32[]{:S(2)}, u32[]{:S(2)}) collective-permute-start(f32[2,128,256]{2,1,0:T(8,128)} %slice.682), channel_id=1, source_target_pairs={{0,1},{1,2},{2,3},{3,4},{4,5},{5,6},{6,7},{8,9},{9,10},{10,11},{11... | collective-permute-start | bytes 786440 | tf_op jit(solution)/shard_map/ppermute | solution.py:17
  249.5 12.7 %collective-permute-start.6 = (f32[2,128,256]{2,1,0:T(8,128)}, f32[2,128,256]{2,1,0:T(8,128)}, u32[]{:S(2)}, u32[]{:S(2)}) collective-permute-start(f32[2,128,256]{2,1,0:T(8,128)} %get-tuple-element.125), channel_id=1, source_target_pairs={{0,1},{1,2},{2,3},{3,4},{4,5},{5,6},{6,7},{8,9},{9,10},{10,11},{11... | collective-permute-start | bytes 786440 | tf_op jit(solution)/shard_map/ppermute | solution.py:17
  252.4 10.0 %collective-permute-start.7 = (f32[2,128,256]{2,1,0:T(8,128)}, f32[2,128,256]{2,1,0:T(8,128)}, u32[]{:S(2)}, u32[]{:S(2)}) collective-permute-start(f32[2,128,256]{2,1,0:T(8,128)} %get-tuple-element.126), channel_id=1, source_target_pairs={{1,0},{2,1},{3,2},{4,3},{5,4},{6,5},{7,6},{9,8},{10,9},{11,10},{12... | collective-permute-start | bytes 786440 | tf_op jit(solution)/shard_map/ppermute | solution.py:19
  273.4 22.8 %collective-permute-start.8 = (f32[2,128,256]{2,1,0:T(8,128)}, f32[2,128,256]{2,1,0:T(8,128)}, u32[]{:S(2)}, u32[]{:S(2)}) collective-permute-start(f32[2,128,256]{2,1,0:T(8,128)} %get-tuple-element.121), channel_id=1, source_target_pairs={{0,1},{1,2},{2,3},{3,4},{4,5},{5,6},{6,7},{8,9},{9,10},{10,11},{11... | collective-permute-start | bytes 786440 | tf_op jit(solution)/shard_map/ppermute | solution.py:17
  277.9 18.3 %collective-permute-start.9 = (f32[2,128,256]{2,1,0:T(8,128)}, f32[2,128,256]{2,1,0:T(8,128)}, u32[]{:S(2)}, u32[]{:S(2)}) collective-permute-start(f32[2,128,256]{2,1,0:T(8,128)} %get-tuple-element.122), channel_id=1, source_target_pairs={{1,0},{2,1},{3,2},{4,3},{5,4},{6,5},{7,6},{9,8},{10,9},{11,10},{12... | collective-permute-start | bytes 786440 | tf_op jit(solution)/shard_map/ppermute | solution.py:19
  281.2 71.5 %collective-permute-start.13 = (f32[2,128,256]{2,1,0:T(8,128)}, f32[2,128,256]{2,1,0:T(8,128)}, u32[]{:S(2)}, u32[]{:S(2)}) collective-permute-start(f32[2,128,256]{2,1,0:T(8,128)} %slice.685), channel_id=1, source_target_pairs={{1,0},{2,1},{3,2},{4,3},{5,4},{6,5},{7,6},{9,8},{10,9},{11,10},{12... | collective-permute-start | bytes 786440 | tf_op jit(solution)/shard_map/ppermute | solution.py:19
  301.9 16.5 %collective-permute-start.10 = (f32[2,128,256]{2,1,0:T(8,128)}, f32[2,128,256]{2,1,0:T(8,128)S(1)}, u32[]{:S(2)}, u32[]{:S(2)}) collective-permute-start(f32[2,128,256]{2,1,0:T(8,128)} %get-tuple-element.119), channel_id=1, source_target_pairs={{0,1},{1,2},{2,3},{3,4},{4,5},{5,6},{6,7},{8,9},{9,10},{10,11},{11... | collective-permute-start | bytes 786440 | tf_op jit(solution)/shard_map/ppermute | solution.py:17
  306.5 11.9 %collective-permute-start.11 = (f32[2,128,256]{2,1,0:T(8,128)}, f32[2,128,256]{2,1,0:T(8,128)}, u32[]{:S(2)}, u32[]{:S(2)}) collective-permute-start(f32[2,128,256]{2,1,0:T(8,128)} %get-tuple-element.120), channel_id=1, source_target_pairs={{1,0},{2,1},{3,2},{4,3},{5,4},{6,5},{7,6},{9,8},{10,9},{11,10},{12... | collective-permute-start | bytes 786440 | tf_op jit(solution)/shard_map/ppermute | solution.py:19
  334.0 17.5 %copy-start.19 = (f32[8,128,256]{2,1,0:T(8,128)S(1)}, f32[8,128,256]{2,1,0:T(8,128)}, u32[]{:S(2)}) copy-start(f32[8,128,256]{2,1,0:T(8,128)} %reshape.382) | copy-start | bytes 3145732
  334.0 25.2 %copy-start.14 = (f32[8,128,256]{2,1,0:T(8,128)S(1)}, f32[8,128,256]{2,1,0:T(8,128)}, u32[]{:S(2)}) copy-start(f32[8,128,256]{2,1,0:T(8,128)} %copy-done.13) | copy-start | bytes 3145732
  334.0 25.2 %copy-start.16 = (f32[8,128,256]{2,1,0:T(8,128)S(1)}, f32[8,128,256]{2,1,0:T(8,128)}, u32[]{:S(2)}) copy-start(f32[8,128,256]{2,1,0:T(8,128)} %copy-done.15) | copy-start | bytes 3145732
  334.0 25.2 %copy-start.18 = (f32[8,128,256]{2,1,0:T(8,128)S(1)}, f32[8,128,256]{2,1,0:T(8,128)}, u32[]{:S(2)}) copy-start(f32[8,128,256]{2,1,0:T(8,128)} %get-tuple-element.81) | copy-start | bytes 3145732
  345.1 8.7 %collective-permute-start.14 = (f32[2,128,256]{2,1,0:T(8,128)S(1)}, f32[2,128,256]{2,1,0:T(8,128)S(1)}, u32[]{:S(2)}, u32[]{:S(2)}) collective-permute-start(f32[2,128,256]{2,1,0:T(8,128)S(1)} %get-tuple-element.117), channel_id=1, source_target_pairs={{0,1},{1,2},{2,3},{3,4},{4,5},{5,6},{6,7},{8,9},{9,10},{10,11},{11... | collective-permute-start | bytes 786440 | tf_op jit(solution)/shard_map/ppermute | solution.py:17
  350.0 9.2 %collective-permute-start.15 = (f32[2,128,256]{2,1,0:T(8,128)S(1)}, f32[2,128,256]{2,1,0:T(8,128)S(1)}, u32[]{:S(2)}, u32[]{:S(2)}) collective-permute-start(f32[2,128,256]{2,1,0:T(8,128)S(1)} %get-tuple-element.118), channel_id=1, source_target_pairs={{1,0},{2,1},{3,2},{4,3},{5,4},{6,5},{7,6},{9,8},{10,9},{11,10},{12... | collective-permute-start | bytes 786440 | tf_op jit(solution)/shard_map/ppermute | solution.py:19
  (30 other events, 166.3 us)
Sparse Core Ops, SparseCore 0:
  11.3 81.8 all-gather.2
  96.6 74.6 all-gather.4
  367.3 277.5 all-reduce.18
where the time goes:
time: 663 us; the launch traced here: 653 us
  waiting for transfers between devices  446 us (67%)
  other arithmetic  82.2 us (12%)
  local copies, waits for them, and re-layouts  65.1 us (10%)
  starting transfers between devices  42.8 us (6%)
  between operations  17.3 us (3%)
    psum x1, waiting for transfers between devices, sum_shots(): whole_one, whole_two = lax.psum((first_term, second_term), 'shot')  278 us
    all_gather x1, waiting for transfers between devices, on_device(): lax.all_gather(epsilon, 'shot', axis=1, tiled=True)  78.1 us
    all_gather x1, waiting for transfers between devices, on_device(): lax.all_gather(velocity, 'shot', axis=1, tiled=True)  65.5 us
    ppermute x8, starting transfers between devices, with_halo(): lax.ppermute(tail, axis, [(i, (i + 1) % count) for i in range(ends)])  32.2 us
    unnamed x85, local copies, waits for them, and re-layouts  26.9 us
    ppermute x8, waiting for transfers between devices, with_halo(): lax.ppermute(head, axis, [((i + 1) % count, i) for i in range(ends)])  24.5 us
    scatter-add x10, other arithmetic, inject(): flattened = field.reshape(-1).at[layer_ids * plane_size + within].add(jnp...  19.5 us
    reshape x10, local copies, waits for them, and re-layouts, inject(): return flattened.reshape(field.shape)  17.5 us
  transfers between devices with their start and end apart: 19, of which 8 were waited for; matrix products, arithmetic and copies ran while one was open for 16% of the time, Pallas kernels for 0%

commit v1 on v0

v1 whole, which is shorter than its diff:
```python
import functools

import jax
import jax.numpy as jnp
from jax import lax
from jax.experimental import pallas as pl
from jax.experimental.pallas import tpu as pltpu
from jax.sharding import PartitionSpec as P

STEPS = 4
ROWS = 32
UP, DOWN = 4.0 / 3.0, 1.0 / 12.0
VMEM = pl.BlockSpec(memory_space=pltpu.VMEM)
SMEM = pl.BlockSpec(memory_space=pltpu.SMEM)


def shape(*dims):
    return jax.ShapeDtypeStruct(dims, jnp.float32)


def call(body, outs, args, scalars=0, scratch=(), out_specs=None, work=1.0):
    specs = [SMEM] * scalars + [VMEM] * (len(args) - scalars)
    size = sum(4 * a.size for a in args) + sum(4 * o.size for o in outs)
    return pl.pallas_call(
        body,
        out_shape=tuple(outs),
        in_specs=specs,
        out_specs=tuple(out_specs or [VMEM] * len(outs)),
        scratch_shapes=list(scratch),
        compiler_params=pltpu.CompilerParams(vmem_limit_bytes=48 * 1024 * 1024),
        cost_estimate=pl.CostEstimate(
            flops=int(work * size * 4), bytes_accessed=size, transcendentals=0
        ),
    )(*args)


def edge_rows(load, start, count):
    parts = []
    low, high = max(start - 8, 0), min(start + ROWS + 8, count)
    body = load(low, high - low)
    blank = jnp.zeros((8, body.shape[1]), jnp.float32)
    if start == 0:
        parts.append(blank)
    parts.append(body)
    if start + ROWS == count:
        parts.append(blank)
    return jnp.concatenate(parts, axis=0) if len(parts) > 1 else body


def lateral(wide, lanes):
    rows, length = wide.shape
    mid = wide[8 : 8 + ROWS]

    def x_at(shift):
        return pltpu.roll(wide, shift % rows, 0)[8 : 8 + ROWS]

    def y_at(shift):
        moved = pltpu.roll(mid, shift % length, 1)
        keep = lanes >= shift if shift > 0 else lanes < length + shift
        return jnp.where(keep, moved, 0.0)

    near = (x_at(1) + x_at(-1)) + (y_at(1) + y_at(-1))
    far = (x_at(2) + x_at(-2)) + (y_at(2) + y_at(-2))
    return UP * near - DOWN * far - 5.0 * mid


def vertical(ext, layer, rows):
    def at(offset):
        return ext[layer + offset, rows, :]

    return UP * (at(1) + at(3)) - DOWN * (at(0) + at(4)) - 2.5 * at(2)


def fill(ext, lo, hi):
    depth = ext.shape[0] - 4
    ext[0:2] = lo[...]
    ext[depth + 2 : depth + 4] = hi[...]


def put_ends(ref, ext_or_val, lo_out, hi_out):
    depth = ref.shape[0]
    lo_out[...] = ref[0:2]
    hi_out[...] = ref[depth - 2 : depth]


def forward_kernel(moment, with_image, last, *refs):
    it = iter(refs)
    info, pulse = next(it), next(it)
    p_now, q_now, lo, hi = next(it), next(it), next(it), next(it)
    if not last:
        p_old, q_old, stiff, stretch = next(it), next(it), next(it), next(it)
    if with_image:
        back, side = next(it), next(it)
    if with_image and last:
        one_in, two_in = next(it), next(it)
    if not last:
        p_out, q_out, lo_out, hi_out = next(it), next(it), next(it), next(it)
    first_out, second_out = next(it), next(it)
    ext = next(it)
    depth, width, length = p_now.shape
    fill(ext, lo, hi)
    lanes = lax.broadcasted_iota(jnp.int32, (ROWS, length), 1)
    place = lax.broadcasted_iota(jnp.int32, (ROWS, length), 0) * length + lanes

    def copy(layer, _):
        ext[layer + 2] = q_now[layer]
        return 0

    lax.fori_loop(0, depth, copy, 0)
    here = info[1] - info[0]
    amount = pulse[0, moment] if not last else 0.0

    def step(layer, _):
        for start in range(0, width, ROWS):
            rows = pl.ds(start, ROWS)
            flat = lateral(edge_rows(lambda s, n: p_now[layer, pl.ds(s, n), :], start, width), lanes)
            deep = vertical(ext, layer, rows)
            if not last:
                k = stiff[layer, rows, :]
                hit = place == here - (layer * width + start) * length
                add = jnp.where(hit, amount, 0.0)
                p = (
                    2.0 * p_now[layer, rows, :]
                    - p_old[layer, rows, :]
                    + k * (stretch[layer, rows, :] * flat + deep)
                )
                q = 2.0 * q_now[layer, rows, :] - q_old[layer, rows, :] + k * (flat + deep)
                p_out[layer, rows, :] = p + add
                q_out[layer, rows, :] = q + add
            if with_image:
                a, b = back[layer, rows, :], side[layer, rows, :]
                one = a * flat
                two = a * deep + b * (flat + deep)
                if last:
                    one = one + one_in[layer, rows, :]
                    two = two + two_in[layer, rows, :]
                first_out[layer, rows, :] = one
                second_out[layer, rows, :] = two
            else:
                first_out[layer, rows, :] = flat
                second_out[layer, rows, :] = deep
        return 0

    lax.fori_loop(0, depth, step, 0)
    if not last:
        put_ends(q_out, None, lo_out, hi_out)


def adjoint_kernel(moment, final, *refs):
    it = iter(refs)
    info, count, cells, which, traces = (next(it) for _ in range(5))
    a_now, b_now, a_old, b_old, stiff, stretch, lo, hi = (next(it) for _ in range(8))
    with_image = moment < 2
    if with_image:
        flat_in, deep_in, one_in, two_in = (next(it) for _ in range(4))
    if final:
        keep_out, send_out = next(it), next(it)
    else:
        a_out, b_out, lo_out, hi_out = (next(it) for _ in range(4))
        if with_image:
            one_out, two_out = next(it), next(it)
    ext = next(it)
    if final:
        a_out, b_out = next(it), next(it)
    depth, width, length = a_now.shape
    fill(ext, lo, hi)
    lanes = lax.broadcasted_iota(jnp.int32, (ROWS, length), 1)

    def weigh(layer, _):
        ext[layer + 2] = stiff[layer] * (a_now[layer] + b_now[layer])
        return 0

    lax.fori_loop(0, depth, weigh, 0)

    def step(layer, _):
        for start in range(0, width, ROWS):
            rows = pl.ds(start, ROWS)

            def weighted(s, n):
                r = pl.ds(s, n)
                return stiff[layer, r, :] * (stretch[layer, r, :] * a_now[layer, r, :] + b_now[layer, r, :])

            flat = lateral(edge_rows(weighted, start, width), lanes)
            deep = vertical(ext, layer, rows)
            a_out[layer, rows, :] = 2.0 * a_now[layer, rows, :] - a_old[layer, rows, :] + flat
            b_out[layer, rows, :] = 2.0 * b_now[layer, rows, :] - b_old[layer, rows, :] + deep
        return 0

    lax.fori_loop(0, depth, step, 0)
    tile_row = lax.broadcasted_iota(jnp.int32, (8, length), 0)
    tile_lane = lax.broadcasted_iota(jnp.int32, (8, length), 1)
    tile_place = tile_row * length + tile_lane

    def drop(n, _):
        cell = cells[n]
        tile = cell // (8 * length)
        layer = tile // (width // 8)
        rows = pl.ds(pl.multiple_of((tile % (width // 8)) * 8, 8), 8)
        add = jnp.where(tile_place == cell % (8 * length), traces[0, moment, which[n]], 0.0)
        a_out[layer, rows, :] = a_out[layer, rows, :] + add
        return 0

    lax.fori_loop(0, count[0], drop, 0)

    if with_image:
        core = info[2]

        def image(layer, _):
            for start in range(0, width, ROWS):
                rows = pl.ds(start, ROWS)
                a, b = a_out[layer, rows, :], b_out[layer, rows, :]
                flat, deep = flat_in[layer, rows, :], deep_in[layer, rows, :]
                one = one_in[layer, rows, :] + a * flat
                two = two_in[layer, rows, :] + a * deep + b * (flat + deep)
                if final:
                    keep_out[layer, rows, :] = jnp.where(core == 0, one, two)
                    send_out[layer, rows, :] = jnp.where(core == 0, two, one)
                else:
                    one_out[layer, rows, :] = one
                    two_out[layer, rows, :] = two
            return 0

        lax.fori_loop(0, depth, image, 0)
    if not final:
        for layer in range(2):
            lo_out[layer] = stiff[layer] * (a_out[layer] + b_out[layer])
            top = depth - 2 + layer
            hi_out[layer] = stiff[top] * (a_out[top] + b_out[top])


def receivers_kernel(info, receivers, count, cells, which):
    size = info[3]
    count[0] = 0

    def look(n, found):
        cell = receivers[0, n] - info[0]
        inside = (cell >= 0) & (cell < size)

        cells[found] = jnp.where(inside, cell, 0)
        which[found] = n
        return found + jnp.where(inside, 1, 0)

    count[0] = lax.fori_loop(0, receivers.shape[1], look, 0)


def quad_kernel(info, vel, eps, from_core, from_side, from_both, out):
    core, side = info[2], info[4]
    rows = vel.shape[1]
    mine = jnp.where(core == 0, vel[...], eps[...])
    for c in range(2):
        near = jnp.where(core == c, mine, from_core[...])
        far = jnp.where(core == c, from_side[...], from_both[...])
        out[:, rows * c : rows * (c + 1), :] = jnp.where(side == 0, near, far)
        out[:, rows * (2 + c) : rows * (3 + c), :] = jnp.where(side == 0, far, near)


def model_kernel(info, *refs):
    own, other = refs[0:9], refs[9:18]
    a_ref, b_ref, stiff, stretch, lo_out, hi_out = refs[18:]
    core, line = info[2], info[5]
    depth, width, length = stiff.shape
    band = own[0].shape[1]
    lines = width // band

    def place(steps):
        return pl.ds(pl.multiple_of(lax.rem(line + steps, lines) * band, band), band)

    steps = (0, 1, 7, 2, 6, 3, 5)
    pieces = [(own[i], other[i], place(s), 0) for i, s in enumerate(steps)]
    pieces += [(own[7], other[7], place(4), 0), (own[8], other[8], place(4), depth // 2)]
    for mine, theirs, rows, first in pieces:
        for layer in range(mine.shape[0]):
            x, y = mine[layer], theirs[layer]
            vel = jnp.where(core == 0, x, y)
            eps = jnp.where(core == 0, y, x)
            stiff[first + layer, rows, :] = vel * vel
            stretch[first + layer, rows, :] = 1.0 + 2.0 * eps
    for layer in range(2):
        lo_out[layer] = stiff[layer] * (a_ref[layer] + b_ref[layer])
        top = depth - 2 + layer
        hi_out[layer] = stiff[top] * (a_ref[top] + b_ref[top])


def split_kernel(info, keep, got, *outs):
    line = info[5]
    width = keep.shape[1]
    band = outs[0].shape[1]
    lines = width // band
    half = keep.shape[0] // 2
    for i, steps in enumerate((0, 1, 7, 2, 6, 3, 5)):
        rows = pl.ds(pl.multiple_of(lax.rem(line + steps, lines) * band, band), band)
        outs[i][...] = keep[:, rows, :] + got[:, rows, :]
    rows = pl.ds(pl.multiple_of(lax.rem(line + 4, lines) * band, band), band)
    outs[7][...] = keep[:half, rows, :] + got[:half, rows, :]
    outs[8][...] = keep[half:, rows, :] + got[half:, rows, :]


def relay_kernel(plus, minus, from_minus, from_plus, low, high, plus_out, minus_out):
    half = low.shape[0]
    plus_out[...] = plus[...] + from_minus[...]
    minus_out[...] = minus[...] + from_plus[...]
    plus_out[0:half] = plus_out[0:half] + low[...]
    minus_out[half:] = minus_out[half:] + high[...]


def lines_kernel(info, own, r1, r2, r3, r4, keep, send):
    side = info[4]
    total = (own[...] + (r1[...] + r2[...])) + (r3[...] + r4[...])
    rows = keep.shape[1]
    keep[...] = jnp.where(side == 0, total[:, :rows], total[:, rows:])
    send[...] = jnp.where(side == 0, total[:, rows:], total[:, :rows])


def sides_kernel(info, keep, got, mine, send):
    core = info[2]
    rows = mine.shape[1]
    low = keep[:, :rows, :] + got[:, :rows, :]
    high = keep[:, rows:, :] + got[:, rows:, :]
    mine[...] = jnp.where(core == 0, low, high)
    send[...] = jnp.where(core == 0, high, low)


def gradient_kernel(info, mine, got, vel, eps, vel_out, eps_out):
    core = info[2]
    one = jnp.where(core == 0, mine[...], got[...])
    two = jnp.where(core == 0, got[...], mine[...])
    v = vel[...]
    vel_out[...] = 2.0 * v * ((1.0 + 2.0 * eps[...]) * one + two)
    eps_out[...] = 2.0 * (v * v) * one


def on_device(
    velocity, epsilon, forward_state, adjoint_state, source_cell, wavelet, receiver_cells, residuals
):
    depth, share, length = velocity.shape
    width = forward_state.shape[3]
    shots = lax.axis_size("shot")
    slabs = lax.axis_size("dom")
    lines = shots // 4
    field = shape(depth, width, length)
    ends = shape(2, width, length)
    shot = lax.axis_index("shot")
    core, side, line = shot % 2, (shot // 2) % 2, shot // 4
    info = jnp.stack(
        [
            lax.axis_index("dom") * (depth * width * length),
            source_cell[0],
            core,
            jnp.int32(depth * width * length),
            side,
            line,
        ]
    ).astype(jnp.int32)

    up = [(i, i + 1) for i in range(slabs - 1)]
    down = [(i + 1, i) for i in range(slabs - 1)]

    def halos(lo, hi):
        return lax.ppermute(hi, "dom", up), lax.ppermute(lo, "dom", down)

    def swap(x, mask):
        return lax.ppermute(x, "shot", [(s, s ^ mask) for s in range(shots)])

    def from_line(x, steps):
        pairs = [(s, ((s // 4 - steps) % lines) * 4 + s % 4) for s in range(shots)]
        return lax.ppermute(x, "shot", pairs)

    p_old, p_now, q_old, q_now = (forward_state[0, i] for i in range(4))
    a_old, a_now, b_old, b_now = (adjoint_state[0, i] for i in range(4))

    mine = jnp.where(core == 0, velocity, epsilon)
    theirs = jnp.where(core == 0, epsilon, velocity)
    from_side = swap(mine, 2)
    from_both = swap(theirs, 3)
    from_core = swap(theirs, 1)
    q_lo, q_hi = halos(q_now[:2], q_now[depth - 2 :])
    quad = call(
        quad_kernel,
        [shape(depth, 4 * share, length)],
        (info, velocity, epsilon, from_core, from_side, from_both),
        1,
    )[0]
    half = depth // 2
    n2, m2 = from_line(quad, 2), from_line(quad, -2)
    n1, m1 = from_line(quad, 1), from_line(quad, -1)
    low, high = from_line(n2[:half], 2), from_line(m2[half:], -2)
    n3, m3 = from_line(n2, 1), from_line(m2, -1)
    own = (quad, n1, m1, n2, m2, n3, m3, low, high)
    other = tuple(swap(x, 1) for x in own)
    stiff, stretch, w_lo, w_hi = call(
        model_kernel, [field, field, ends, ends], (info, *own, *other, a_now, b_now), 1
    )
    spots = jax.ShapeDtypeStruct((receiver_cells.shape[1] + 1,), jnp.int32)
    count, cells, which = call(
        receivers_kernel,
        [jax.ShapeDtypeStruct((1,), jnp.int32), spots, spots],
        (info, receiver_cells),
        2,
        out_specs=[SMEM] * 3,
    )
    ext = pltpu.VMEM((depth + 4, width, length), jnp.float32)
    plane = pltpu.VMEM((depth, width, length), jnp.float32)

    def forward(moment, extra, with_image, last, outs):
        return call(
            functools.partial(forward_kernel, moment, with_image, last),
            outs,
            (info, wavelet, p_now, q_now, q_lo, q_hi, *extra),
            2,
            [ext],
        )

    def adjoint(moment, extra, final, outs):
        return call(
            functools.partial(adjoint_kernel, moment, final),
            outs,
            (info, count, cells, which, residuals, a_now, b_now, a_old, b_old, stiff, stretch, w_lo, w_hi, *extra),
            5,
            [ext] + ([plane, plane] if final else []),
        )

    six = [field, field, ends, ends, field, field]
    flats, deeps = [], []
    w_lo, w_hi = halos(w_lo, w_hi)
    p_new, q_new, lo, hi, flat, deep = forward(0, (p_old, q_old, stiff, stretch), False, False, six)
    flats.append(flat)
    deeps.append(deep)
    p_old, p_now, q_old, q_now = p_now, p_new, q_now, q_new
    q_lo, q_hi = halos(lo, hi)

    a_new, b_new, lo, hi = adjoint(3, (), False, six[:4])
    a_old, a_now, b_old, b_now = a_now, a_new, b_now, b_new
    a_four, b_four = a_new, b_new
    w_lo, w_hi = halos(lo, hi)

    p_new, q_new, lo, hi, flat, deep = forward(1, (p_old, q_old, stiff, stretch), False, False, six)
    flats.append(flat)
    deeps.append(deep)
    p_old, p_now, q_old, q_now = p_now, p_new, q_now, q_new
    q_lo, q_hi = halos(lo, hi)

    a_new, b_new, lo, hi = adjoint(2, (), False, six[:4])
    a_old, a_now, b_old, b_now = a_now, a_new, b_now, b_new
    w_lo, w_hi = halos(lo, hi)

    p_new, q_new, lo, hi, one, two = forward(2, (p_old, q_old, stiff, stretch, a_now, b_now), True, False, six)
    p_old, p_now, q_old, q_now = p_now, p_new, q_now, q_new
    q_lo, q_hi = halos(lo, hi)

    a_new, b_new, lo, hi, one, two = adjoint(1, (flats[1], deeps[1], one, two), False, six)
    a_old, a_now, b_old, b_now = a_now, a_new, b_now, b_new
    w_lo, w_hi = halos(lo, hi)

    one, two = forward(3, (a_four, b_four, one, two), True, True, [field, field])
    keep, send = adjoint(0, (flats[0], deeps[0], one, two), True, [field, field])

    band = shape(depth, 4 * share, length)
    half_band = shape(half, 4 * share, length)
    got = swap(send, 1)
    own, s1, t1, s2, t2, s3, t3, low, high = call(
        split_kernel, [band] * 7 + [half_band] * 2, (info, keep, got), 1
    )
    g3, h3 = from_line(s3, -1), from_line(t3, 1)
    g4, h4 = from_line(low, -2), from_line(high, 2)
    s2, t2 = call(relay_kernel, [band] * 2, (s2, t2, g3, h3, g4, h4))
    got = [from_line(s2, -2), from_line(t2, 2), from_line(s1, -1), from_line(t1, 1)]
    pair = shape(depth, 2 * share, length)
    keep, send = call(lines_kernel, [pair, pair], (info, own, *got), 1)
    keep, send = call(
        sides_kernel, [shape(depth, share, length)] * 2, (info, keep, swap(send, 2)), 1
    )
    vel_grad, eps_grad = call(
        gradient_kernel,
        [shape(depth, share, length)] * 2,
        (info, keep, swap(send, 1), velocity, epsilon),
        1,
    )
    return vel_grad, eps_grad


def solution(mesh):
    placed = (
        P("dom", "shot", None),
        P("dom", "shot", None),
        P("shot", None, "dom", None, None),
        P("shot", None, "dom", None, None),
        P("shot"),
        P("shot", None),
        P("shot", None),
        P("shot", None, None),
    )
    return jax.shard_map(
        on_device,
        mesh=mesh,
        in_specs=placed,
        out_specs=(P("dom", "shot", None), P("dom", "shot", None)),
        check_vma=False,
    )
```

time: 663 us -> 198 us (0.30); the launches traced: 653 us -> 197 us
  waiting for transfers between devices: 446 us -> 21.5 us
  other arithmetic: 82.2 us -> 0.78 us
  Pallas kernels: 0 us -> 55.3 us
  starting transfers between devices: 42.8 us -> 96.4 us
  local copies, waits for them, and re-layouts: 65.1 us -> 20.7 us
  between operations: 17.3 us -> 1.97 us
    psum x1 -> x0, waiting for transfers between devices: 278 us -> none  [sum_shots(): whole_one, whole_two = lax.psum((first_term, second_term), 'shot')]
    all_gather x2 -> x0, waiting for transfers between devices: 144 us -> none  [the longest x1 78.1 us: on_device(): lax.all_gather(epsilon, 'shot', axis=1, tiled=True)]
    pallas_call x0 -> x16, Pallas kernels: none -> 55.3 us  [call(): pl.pallas_call(body, out_shape=tuple(outs), in_specs=specs, out_specs=tup...]
    ppermute x16 -> x47, starting transfers between devices: 42.7 us -> 96.4 us  [the longest x16 45.8 us: halos(): return (lax.ppermute(hi, 'dom', up), lax.ppermute(lo, 'dom', down))]
    mul x8 -> x0, other arithmetic: 43.6 us -> none  [the longest x3 13.8 us: on_device(): stiffness * (back_now + side_now)]
    scatter-add x10 -> x0, other arithmetic: 19.5 us -> none  [inject(): flattened = field.reshape(-1).at[layer_ids * plane_size + within].add(jnp...]
    add x8 -> x0, other arithmetic: 19.2 us -> none  [the longest x2 9.43 us: on_device(): 2.0 * pressure_now - pressure_old]
    reshape x10 -> x0, local copies, waits for them, and re-layouts: 17.5 us -> none  [inject(): return flattened.reshape(field.shape)]
  transfers between devices with their start and end apart: 19 -> 47, of which waited for: 8 -> 11; matrix products, arithmetic and copies ran while one was open for 16% -> 3% of each run, Pallas kernels for 0% -> 23%
where the time goes in v1:
time: 198 us; the launch traced here: 197 us
  starting transfers between devices  96.4 us (49%)
  Pallas kernels  55.3 us (28%)
  waiting for transfers between devices  21.5 us (11%)
  local copies, waits for them, and re-layouts  20.7 us (10%)
    pallas_call x16, Pallas kernels, call(): pl.pallas_call(body, out_shape=tuple(outs), in_specs=specs, out_specs=tup...  55.3 us
    ppermute x16, starting transfers between devices, halos(): return (lax.ppermute(hi, 'dom', up), lax.ppermute(lo, 'dom', down))  45.8 us
    ppermute x16, starting transfers between devices, from_line(): return lax.ppermute(x, 'shot', pairs)  30.1 us
    ppermute x15, starting transfers between devices, swap(): return lax.ppermute(x, 'shot', [(s, s ^ mask) for s in range(shots)])  20.5 us
    unnamed x64, local copies, waits for them, and re-layouts  14.6 us
    ppermute x16, waiting for transfers between devices, from_line(): return lax.ppermute(x, 'shot', pairs)  10.5 us
    ppermute x15, waiting for transfers between devices, swap(): return lax.ppermute(x, 'shot', [(s, s ^ mask) for s in range(shots)])  9.02 us
  transfers between devices with their start and end apart: 47, of which 11 were waited for; matrix products, arithmetic and copies ran while one was open for 3% of the time, Pallas kernels for 23%

profile of v1, /device:TPU:1, one launch (start us, length us, event | category | flops | bytes accessed | tf_op | source)
XLA Modules:
  0.0 196.6 jit_solution(232563016789122462)
XLA Ops:
  1.4 3.6 %collective-permute-start.1 = (f32[8,4,256]{2,1,0:T(4,128)S(1)}, f32[8,4,256]{2,1,0:T(4,128)S(1)}, u32[]{:S(2)}, u32[]{:S(2)}) collective-permute-start(f32[8,4,256]{2,1,0:T(4,128)S(1)} %bitcast.32), channel_id=1, source_target_pairs={{0,16},{8,24},{16,0},{24,8},{32,48},{40,56},{48,32},{56,40},{64,80... | collective-permute-start | bytes 98312 | tf_op jit(solution)/shard_map/ppermute | solution.py:362
  16.0 3.1 %collective-permute-start.5 = (f32[8,16,256]{2,1,0:T(8,128)S(1)}, f32[8,16,256]{2,1,0:T(8,128)S(1)}, u32[]{:S(2)}, u32[]{:S(2)}) collective-permute-start(f32[8,16,256]{2,1,0:T(8,128)S(1)} %shard_map.96.refs_0_), channel_id=1, source_target_pairs={{0,192},{8,200},{16,208},{24,216},{32,224},{40,232},{48,240},{56,2... | collective-permute-start | bytes 393224 | tf_op jit(solution)/shard_map/ppermute | solution.py:366
  34.8 4.0 %slice_bitcast_fusion.4 = (f32[8,128,256]{2,1,0:T(8,128)}, f32[8,128,256]{2,1,0:T(8,128)}, f32[8,128,256]{2,1,0:T(8,128)S(1)}, f32[8,128,256]{2,1,0:T(8,128)}) fusion(f32[1,4,8,128,256]{4,3,2,1,0:T(8,128)} %param.11), kind=kLoop, calls=%fused_computation.4 | loop fusion | bytes 8388608 | tf_op jit(solution)/shard_map/squeeze | solution.py:369
  41.4 4.0 %collective-permute-start.26 = (f32[2,128,256]{2,1,0:T(8,128)S(1)}, f32[2,128,256]{2,1,0:T(8,128)S(1)}, u32[]{:S(2)}, u32[]{:S(2)}) collective-permute-start(f32[2,128,256]{2,1,0:T(8,128)S(1)} %get-tuple-element.123), channel_id=1, source_target_pairs={{0,1},{1,2},{2,3},{3,4},{4,5},{5,6},{6,7},{8,9},{9,10},{10,11},{11... | collective-permute-start | bytes 786440 | tf_op jit(solution)/shard_map/ppermute | solution.py:359
  47.0 3.1 %collective-permute-start.20 = (f32[2,128,256]{2,1,0:T(8,128)S(1)}, f32[2,128,256]{2,1,0:T(8,128)S(1)}, u32[]{:S(2)}, u32[]{:S(2)}) collective-permute-start(f32[2,128,256]{2,1,0:T(8,128)S(1)} %get-tuple-element.65), channel_id=1, source_target_pairs={{0,1},{1,2},{2,3},{3,4},{4,5},{5,6},{6,7},{8,9},{9,10},{10,11},{11... | collective-permute-start | bytes 786440 | tf_op jit(solution)/shard_map/ppermute | solution.py:359
  53.5 5.1 %shard_map.100 = (f32[8,128,256]{2,1,0:T(8,128)S(1)}, f32[8,128,256]{2,1,0:T(8,128)S(1)}, f32[2,128,256]{2,1,0:T(8,128)S(1)}, f32[2,128,256]{2,1,0:T(8,128)S(1)}...) custom-call(s32[6]{0:T(128)S(1)} %stack.19.info.refs_0_, f32[1,3]{1,0:T(1,128)S(1)} %copy-done.29, ...), custom_call_target="tpu_custom_call" | custom-call | flops 46137488 | bytes 11534372 | tf_op jit(solution)/shard_map/pallas_call | solution.py:24
  60.6 4.0 %collective-permute-start.28 = (f32[2,128,256]{2,1,0:T(8,128)S(1)}, f32[2,128,256]{2,1,0:T(8,128)S(1)}, u32[]{:S(2)}, u32[]{:S(2)}) collective-permute-start(f32[2,128,256]{2,1,0:T(8,128)S(1)} %get-tuple-element.77), channel_id=1, source_target_pairs={{0,1},{1,2},{2,3},{3,4},{4,5},{5,6},{6,7},{8,9},{9,10},{10,11},{11... | collective-permute-start | bytes 786440 | tf_op jit(solution)/shard_map/ppermute | solution.py:359
  65.9 3.6 %shard_map.95 = (s32[1]{0:T(128)}, s32[257]{0:T(512)S(1)}, s32[257]{0:T(512)S(1)}) custom-call(s32[6]{0:T(128)S(1)} %stack.19.info.refs_0_, s32[1,256]{1,0:T(1,128)S(1)} %copy-done.30), custom_call_target="tpu_custom_call" | custom-call | flops 12432 | bytes 3108 | tf_op jit(solution)/shard_map/pallas_call | solution.py:24
  69.6 5.8 %shard_map.98 = (f32[8,128,256]{2,1,0:T(8,128)S(1)}, f32[8,128,256]{2,1,0:T(8,128)S(1)}, f32[2,128,256]{2,1,0:T(8,128)S(1)}, f32[2,128,256]{2,1,0:T(8,128)S(1)}) custom-call(s32[6]{0:T(128)S(1)} %stack.19.info.refs_0_, s32[1]{0:T(128)} %get-tuple-element.60.refs_1_, s32[257]{0:T(512)S(1)} %get-tuple-element.61.refs_2_, s32[257]{0:T(512)S(1)} %get-tuple-element.62.refs_3_, ...), custom_call_target="tpu_custom_call" | custom-call | flops 37773456 | bytes 9443364 | tf_op jit(solution)/shard_map/pallas_call | solution.py:24
  75.5 4.9 %collective-permute-start.22 = (f32[2,128,256]{2,1,0:T(8,128)S(1)}, f32[2,128,256]{2,1,0:T(8,128)S(1)}, u32[]{:S(2)}, u32[]{:S(2)}) collective-permute-start(f32[2,128,256]{2,1,0:T(8,128)S(1)} %get-tuple-element.69), channel_id=1, source_target_pairs={{0,1},{1,2},{2,3},{3,4},{4,5},{5,6},{6,7},{8,9},{9,10},{10,11},{11... | collective-permute-start | bytes 786440 | tf_op jit(solution)/shard_map/ppermute | solution.py:359
  81.7 5.0 %shard_map.101 = (f32[8,128,256]{2,1,0:T(8,128)S(1)}, f32[8,128,256]{2,1,0:T(8,128)S(1)}, f32[2,128,256]{2,1,0:T(8,128)S(1)}, f32[2,128,256]{2,1,0:T(8,128)S(1)}...) custom-call(s32[6]{0:T(128)S(1)} %stack.19.info.refs_0_, f32[1,3]{1,0:T(1,128)S(1)} %copy-done.29, ...), custom_call_target="tpu_custom_call" | custom-call | flops 46137488 | bytes 11534372 | tf_op jit(solution)/shard_map/pallas_call | solution.py:24
  89.7 4.7 %collective-permute-start.30 = (f32[2,128,256]{2,1,0:T(8,128)S(1)}, f32[2,128,256]{2,1,0:T(8,128)S(1)}, u32[]{:S(2)}, u32[]{:S(2)}) collective-permute-start(f32[2,128,256]{2,1,0:T(8,128)S(1)} %get-tuple-element.83), channel_id=1, source_target_pairs={{0,1},{1,2},{2,3},{3,4},{4,5},{5,6},{6,7},{8,9},{9,10},{10,11},{11... | collective-permute-start | bytes 786440 | tf_op jit(solution)/shard_map/ppermute | solution.py:359
  95.7 5.8 %shard_map.99 = (f32[8,128,256]{2,1,0:T(8,128)S(1)}, f32[8,128,256]{2,1,0:T(8,128)S(1)}, f32[2,128,256]{2,1,0:T(8,128)S(1)}, f32[2,128,256]{2,1,0:T(8,128)S(1)}) custom-call(s32[6]{0:T(128)S(1)} %stack.19.info.refs_0_, s32[1]{0:T(128)} %get-tuple-element.60.refs_1_, s32[257]{0:T(512)S(1)} %get-tuple-element.61.refs_2_, s32[257]{0:T(512)S(1)} %get-tuple-element.62.refs_3_, ...), custom_call_target="tpu_custom_call" | custom-call | flops 37773456 | bytes 9443364 | tf_op jit(solution)/shard_map/pallas_call | solution.py:24
  103.5 5.0 %collective-permute-start.24 = (f32[2,128,256]{2,1,0:T(8,128)S(1)}, f32[2,128,256]{2,1,0:T(8,128)S(1)}, u32[]{:S(2)}, u32[]{:S(2)}) collective-permute-start(f32[2,128,256]{2,1,0:T(8,128)S(1)} %get-tuple-element.73), channel_id=1, source_target_pairs={{0,1},{1,2},{2,3},{3,4},{4,5},{5,6},{6,7},{8,9},{9,10},{10,11},{11... | collective-permute-start | bytes 786440 | tf_op jit(solution)/shard_map/ppermute | solution.py:359
  109.9 5.8 %shard_map.102 = (f32[8,128,256]{2,1,0:T(8,128)S(1)}, f32[8,128,256]{2,1,0:T(8,128)S(1)}, f32[2,128,256]{2,1,0:T(8,128)S(1)}, f32[2,128,256]{2,1,0:T(8,128)S(1)}...) custom-call(s32[6]{0:T(128)S(1)} %stack.19.info.refs_0_, f32[1,3]{1,0:T(1,128)S(1)} %copy-done.29, ...), custom_call_target="tpu_custom_call" | custom-call | flops 54526096 | bytes 13631524 | tf_op jit(solution)/shard_map/pallas_call | solution.py:24
  117.7 4.7 %collective-permute-start.34 = (f32[2,128,256]{2,1,0:T(8,128)S(1)}, f32[2,128,256]{2,1,0:T(8,128)S(1)}, u32[]{:S(2)}, u32[]{:S(2)}) collective-permute-start(f32[2,128,256]{2,1,0:T(8,128)S(1)} %get-tuple-element.95), channel_id=1, source_target_pairs={{0,1},{1,2},{2,3},{3,4},{4,5},{5,6},{6,7},{8,9},{9,10},{10,11},{11... | collective-permute-start | bytes 786440 | tf_op jit(solution)/shard_map/ppermute | solution.py:359
  123.7 8.1 %shard_map.103 = (f32[8,128,256]{2,1,0:T(8,128)S(1)}, f32[8,128,256]{2,1,0:T(8,128)S(1)}, f32[2,128,256]{2,1,0:T(8,128)S(1)}, f32[2,128,256]{2,1,0:T(8,128)S(1)}...) custom-call(s32[6]{0:T(128)S(1)} %stack.19.info.refs_0_, s32[1]{0:T(128)} %get-tuple-element.60.refs_1_, ...), custom_call_target="tpu_custom_call" | custom-call | flops 62939280 | bytes 15734820 | tf_op jit(solution)/shard_map/pallas_call | solution.py:24
  133.8 5.2 %collective-permute-start.32 = (f32[2,128,256]{2,1,0:T(8,128)S(1)}, f32[2,128,256]{2,1,0:T(8,128)S(1)}, u32[]{:S(2)}, u32[]{:S(2)}) collective-permute-start(f32[2,128,256]{2,1,0:T(8,128)S(1)} %get-tuple-element.89), channel_id=1, source_target_pairs={{0,1},{1,2},{2,3},{3,4},{4,5},{5,6},{6,7},{8,9},{9,10},{10,11},{11... | collective-permute-start | bytes 786440 | tf_op jit(solution)/shard_map/ppermute | solution.py:359
  140.3 3.8 %shard_map.104 = (f32[8,128,256]{2,1,0:T(8,128)S(1)}, f32[8,128,256]{2,1,0:T(8,128)S(1)}) custom-call(s32[6]{0:T(128)S(1)} %stack.19.info.refs_0_, f32[1,3]{1,0:T(1,128)S(1)} %copy-done.29, f32[8,128,256]{2,1,0:T(8,128)S(1)} %get-tuple-element.93.refs_2_, f32[8,128,256]{2,1,0:T(8,128)S(1)} %get-tuple-element.94.refs_3_, ...), custom_call_target="tpu_custom_call" | custom-call | flops 35651728 | bytes 8912932 | tf_op jit(solution)/shard_map/pallas_call | solution.py:24
  148.2 7.1 %shard_map.105 = (f32[8,128,256]{2,1,0:T(8,128)S(1)}, f32[8,128,256]{2,1,0:T(8,128)S(1)}) custom-call(s32[6]{0:T(128)S(1)} %stack.19.info.refs_0_, s32[1]{0:T(128)} %get-tuple-element.60.refs_1_, s32[257]{0:T(512)S(1)} %get-tuple-element.61.refs_2_, s32[257]{0:T(512)S(1)} %get-tuple-element.62.refs_3_, f32[1,4,256]{2,1,0:T(4,128)S(1)} %copy-done.28, ...), custom_call_target="tpu_custom_call" | custom-call | flops 52453520 | bytes 13113380 | tf_op jit(solution)/shard_map/pallas_call | solution.py:24
  155.3 5.8 %collective-permute-start.36 = (f32[8,128,256]{2,1,0:T(8,128)S(1)}, f32[8,128,256]{2,1,0:T(8,128)S(1)}, u32[]{:S(2)}, u32[]{:S(2)}) collective-permute-start(f32[8,128,256]{2,1,0:T(8,128)S(1)} %get-tuple-element.102), channel_id=1, source_target_pairs={{0,8},{8,0},{16,24},{24,16},{32,40},{40,32},{48,56},{56,48},{64,72... | collective-permute-start | bytes 3145736 | tf_op jit(solution)/shard_map/ppermute | solution.py:362
  166.8 3.7 %collective-permute-start.39 = (f32[4,16,256]{2,1,0:T(8,128)S(1)}, f32[4,16,256]{2,1,0:T(8,128)S(1)}, u32[]{:S(2)}, u32[]{:S(2)}) collective-permute-start(f32[4,16,256]{2,1,0:T(8,128)S(1)} %get-tuple-element.108), channel_id=1, source_target_pairs={{0,64},{8,72},{16,80},{24,88},{32,96},{40,104},{48,112},{56,120},{... | collective-permute-start | bytes 196616 | tf_op jit(solution)/shard_map/ppermute | solution.py:366
  180.5 4.8 %collective-permute-done.41.r1 = f32[8,16,256]{2,1,0:T(8,128)S(1)} collective-permute-done((f32[8,16,256]{2,1,0:T(8,128)S(1)}, f32[8,16,256]{2,1,0:T(8,128)S(1)}, u32[]{:S(2)}, u32[]{:S(2)}) %collective-permute-start.41) | collective-permute-done | bytes 131104 | tf_op jit(solution)/shard_map/ppermute | solution.py:366
  187.7 3.6 %collective-permute-done.45.got = f32[8,8,256]{2,1,0:T(8,128)S(1)} collective-permute-done((f32[8,8,256]{2,1,0:T(8,128)S(1)}, f32[8,8,256]{2,1,0:T(8,128)S(1)}, u32[]{:S(2)}, u32[]{:S(2)}) %collective-permute-start.45) | collective-permute-done | bytes 65568 | tf_op jit(solution)/shard_map/ppermute | solution.py:362
  (157 shorter events, 80.5 us)
Async XLA Ops:
  12.9 10.6 %collective-permute-start.6 = (f32[8,16,256]{2,1,0:T(8,128)S(1)}, f32[8,16,256]{2,1,0:T(8,128)S(1)}, u32[]{:S(2)}, u32[]{:S(2)}) collective-permute-start(f32[8,16,256]{2,1,0:T(8,128)S(1)} %shard_map.96.refs_0_), channel_id=1, source_target_pairs={{0,64},{8,72},{16,80},{24,88},{32,96},{40,104},{48,112},{56,120},{... | collective-permute-start | bytes 393224 | tf_op jit(solution)/shard_map/ppermute | solution.py:366
  16.0 10.7 %collective-permute-start.5 = (f32[8,16,256]{2,1,0:T(8,128)S(1)}, f32[8,16,256]{2,1,0:T(8,128)S(1)}, u32[]{:S(2)}, u32[]{:S(2)}) collective-permute-start(f32[8,16,256]{2,1,0:T(8,128)S(1)} %shard_map.96.refs_0_), channel_id=1, source_target_pairs={{0,192},{8,200},{16,208},{24,216},{32,224},{40,232},{48,240},{56,2... | collective-permute-start | bytes 393224 | tf_op jit(solution)/shard_map/ppermute | solution.py:366
  19.1 10.1 %collective-permute-start.11 = (f32[8,16,256]{2,1,0:T(8,128)S(1)}, f32[8,16,256]{2,1,0:T(8,128)S(1)}, u32[]{:S(2)}, u32[]{:S(2)}) collective-permute-start(f32[8,16,256]{2,1,0:T(8,128)S(1)} %shard_map.96.refs_0_), channel_id=1, source_target_pairs={{0,8},{8,0},{16,24},{24,16},{32,40},{40,32},{48,56},{56,48},{64,72... | collective-permute-start | bytes 393224 | tf_op jit(solution)/shard_map/ppermute | solution.py:362
  19.4 11.4 %collective-permute-start.4 = (f32[8,16,256]{2,1,0:T(8,128)S(1)}, f32[8,16,256]{2,1,0:T(8,128)S(1)}, u32[]{:S(2)}, u32[]{:S(2)}) collective-permute-start(f32[8,16,256]{2,1,0:T(8,128)S(1)} %shard_map.96.refs_0_), channel_id=1, source_target_pairs={{0,32},{8,40},{16,48},{24,56},{32,64},{40,72},{48,80},{56,88},{64,... | collective-permute-start | bytes 393224 | tf_op jit(solution)/shard_map/ppermute | solution.py:366
  20.1 11.3 %collective-permute-start.3 = (f32[8,16,256]{2,1,0:T(8,128)S(1)}, f32[8,16,256]{2,1,0:T(8,128)S(1)}, u32[]{:S(2)}, u32[]{:S(2)}) collective-permute-start(f32[8,16,256]{2,1,0:T(8,128)S(1)} %shard_map.96.refs_0_), channel_id=1, source_target_pairs={{0,224},{8,232},{16,240},{24,248},{32,0},{40,8},{48,16},{56,24},{6... | collective-permute-start | bytes 393224 | tf_op jit(solution)/shard_map/ppermute | solution.py:366
  29.1 9.6 %collective-permute-start.15 = (f32[8,16,256]{2,1,0:T(8,128)S(1)}, f32[8,16,256]{2,1,0:T(8,128)S(1)}, u32[]{:S(2)}, u32[]{:S(2)}) collective-permute-start(f32[8,16,256]{2,1,0:T(8,128)S(1)} %collective-permute-done.6.refs_4_), channel_id=1, source_target_pairs={{0,8},{8,0},{16,24},{24,16},{32,40},{40,32},{48,56},{56,48},{64,72... | collective-permute-start | bytes 393224 | tf_op jit(solution)/shard_map/ppermute | solution.py:362
  40.1 13.4 %collective-permute-start.27 = (f32[2,128,256]{2,1,0:T(8,128)S(1)}, f32[2,128,256]{2,1,0:T(8,128)S(1)}, u32[]{:S(2)}, u32[]{:S(2)}) collective-permute-start(f32[2,128,256]{2,1,0:T(8,128)S(1)} %get-tuple-element.122), channel_id=1, source_target_pairs={{1,0},{2,1},{3,2},{4,3},{5,4},{6,5},{7,6},{9,8},{10,9},{11,10},{12... | collective-permute-start | bytes 786440 | tf_op jit(solution)/shard_map/ppermute | solution.py:359
  41.4 12.1 %collective-permute-start.26 = (f32[2,128,256]{2,1,0:T(8,128)S(1)}, f32[2,128,256]{2,1,0:T(8,128)S(1)}, u32[]{:S(2)}, u32[]{:S(2)}) collective-permute-start(f32[2,128,256]{2,1,0:T(8,128)S(1)} %get-tuple-element.123), channel_id=1, source_target_pairs={{0,1},{1,2},{2,3},{3,4},{4,5},{5,6},{6,7},{8,9},{9,10},{10,11},{11... | collective-permute-start | bytes 786440 | tf_op jit(solution)/shard_map/ppermute | solution.py:359
  47.0 22.6 %collective-permute-start.20 = (f32[2,128,256]{2,1,0:T(8,128)S(1)}, f32[2,128,256]{2,1,0:T(8,128)S(1)}, u32[]{:S(2)}, u32[]{:S(2)}) collective-permute-start(f32[2,128,256]{2,1,0:T(8,128)S(1)} %get-tuple-element.65), channel_id=1, source_target_pairs={{0,1},{1,2},{2,3},{3,4},{4,5},{5,6},{6,7},{8,9},{9,10},{10,11},{11... | collective-permute-start | bytes 786440 | tf_op jit(solution)/shard_map/ppermute | solution.py:359
  50.1 19.5 %collective-permute-start.21 = (f32[2,128,256]{2,1,0:T(8,128)S(1)}, f32[2,128,256]{2,1,0:T(8,128)S(1)}, u32[]{:S(2)}, u32[]{:S(2)}) collective-permute-start(f32[2,128,256]{2,1,0:T(8,128)S(1)} %get-tuple-element.66), channel_id=1, source_target_pairs={{1,0},{2,1},{3,2},{4,3},{5,4},{6,5},{7,6},{9,8},{10,9},{11,10},{12... | collective-permute-start | bytes 786440 | tf_op jit(solution)/shard_map/ppermute | solution.py:359
  60.6 21.0 %collective-permute-start.28 = (f32[2,128,256]{2,1,0:T(8,128)S(1)}, f32[2,128,256]{2,1,0:T(8,128)S(1)}, u32[]{:S(2)}, u32[]{:S(2)}) collective-permute-start(f32[2,128,256]{2,1,0:T(8,128)S(1)} %get-tuple-element.77), channel_id=1, source_target_pairs={{0,1},{1,2},{2,3},{3,4},{4,5},{5,6},{6,7},{8,9},{9,10},{10,11},{11... | collective-permute-start | bytes 786440 | tf_op jit(solution)/shard_map/ppermute | solution.py:359
  64.6 17.1 %collective-permute-start.29 = (f32[2,128,256]{2,1,0:T(8,128)S(1)}, f32[2,128,256]{2,1,0:T(8,128)S(1)}, u32[]{:S(2)}, u32[]{:S(2)}) collective-permute-start(f32[2,128,256]{2,1,0:T(8,128)S(1)} %get-tuple-element.78), channel_id=1, source_target_pairs={{1,0},{2,1},{3,2},{4,3},{5,4},{6,5},{7,6},{9,8},{10,9},{11,10},{12... | collective-permute-start | bytes 786440 | tf_op jit(solution)/shard_map/ppermute | solution.py:359
  75.5 20.2 %collective-permute-start.22 = (f32[2,128,256]{2,1,0:T(8,128)S(1)}, f32[2,128,256]{2,1,0:T(8,128)S(1)}, u32[]{:S(2)}, u32[]{:S(2)}) collective-permute-start(f32[2,128,256]{2,1,0:T(8,128)S(1)} %get-tuple-element.69), channel_id=1, source_target_pairs={{0,1},{1,2},{2,3},{3,4},{4,5},{5,6},{6,7},{8,9},{9,10},{10,11},{11... | collective-permute-start | bytes 786440 | tf_op jit(solution)/shard_map/ppermute | solution.py:359
  80.4 15.3 %collective-permute-start.23 = (f32[2,128,256]{2,1,0:T(8,128)S(1)}, f32[2,128,256]{2,1,0:T(8,128)S(1)}, u32[]{:S(2)}, u32[]{:S(2)}) collective-permute-start(f32[2,128,256]{2,1,0:T(8,128)S(1)} %get-tuple-element.70), channel_id=1, source_target_pairs={{1,0},{2,1},{3,2},{4,3},{5,4},{6,5},{7,6},{9,8},{10,9},{11,10},{12... | collective-permute-start | bytes 786440 | tf_op jit(solution)/shard_map/ppermute | solution.py:359
  89.7 20.2 %collective-permute-start.30 = (f32[2,128,256]{2,1,0:T(8,128)S(1)}, f32[2,128,256]{2,1,0:T(8,128)S(1)}, u32[]{:S(2)}, u32[]{:S(2)}) collective-permute-start(f32[2,128,256]{2,1,0:T(8,128)S(1)} %get-tuple-element.83), channel_id=1, source_target_pairs={{0,1},{1,2},{2,3},{3,4},{4,5},{5,6},{6,7},{8,9},{9,10},{10,11},{11... | collective-permute-start | bytes 786440 | tf_op jit(solution)/shard_map/ppermute | solution.py:359
  94.4 15.5 %collective-permute-start.31 = (f32[2,128,256]{2,1,0:T(8,128)S(1)}, f32[2,128,256]{2,1,0:T(8,128)S(1)}, u32[]{:S(2)}, u32[]{:S(2)}) collective-permute-start(f32[2,128,256]{2,1,0:T(8,128)S(1)} %get-tuple-element.84), channel_id=1, source_target_pairs={{1,0},{2,1},{3,2},{4,3},{5,4},{6,5},{7,6},{9,8},{10,9},{11,10},{12... | collective-permute-start | bytes 786440 | tf_op jit(solution)/shard_map/ppermute | solution.py:359
  103.5 20.1 %collective-permute-start.24 = (f32[2,128,256]{2,1,0:T(8,128)S(1)}, f32[2,128,256]{2,1,0:T(8,128)S(1)}, u32[]{:S(2)}, u32[]{:S(2)}) collective-permute-start(f32[2,128,256]{2,1,0:T(8,128)S(1)} %get-tuple-element.73), channel_id=1, source_target_pairs={{0,1},{1,2},{2,3},{3,4},{4,5},{5,6},{6,7},{8,9},{9,10},{10,11},{11... | collective-permute-start | bytes 786440 | tf_op jit(solution)/shard_map/ppermute | solution.py:359
  108.6 15.1 %collective-permute-start.25 = (f32[2,128,256]{2,1,0:T(8,128)S(1)}, f32[2,128,256]{2,1,0:T(8,128)S(1)}, u32[]{:S(2)}, u32[]{:S(2)}) collective-permute-start(f32[2,128,256]{2,1,0:T(8,128)S(1)} %get-tuple-element.74), channel_id=1, source_target_pairs={{1,0},{2,1},{3,2},{4,3},{5,4},{6,5},{7,6},{9,8},{10,9},{11,10},{12... | collective-permute-start | bytes 786440 | tf_op jit(solution)/shard_map/ppermute | solution.py:359
  117.7 22.6 %collective-permute-start.34 = (f32[2,128,256]{2,1,0:T(8,128)S(1)}, f32[2,128,256]{2,1,0:T(8,128)S(1)}, u32[]{:S(2)}, u32[]{:S(2)}) collective-permute-start(f32[2,128,256]{2,1,0:T(8,128)S(1)} %get-tuple-element.95), channel_id=1, source_target_pairs={{0,1},{1,2},{2,3},{3,4},{4,5},{5,6},{6,7},{8,9},{9,10},{10,11},{11... | collective-permute-start | bytes 786440 | tf_op jit(solution)/shard_map/ppermute | solution.py:359
  122.3 17.9 %collective-permute-start.35 = (f32[2,128,256]{2,1,0:T(8,128)S(1)}, f32[2,128,256]{2,1,0:T(8,128)S(1)}, u32[]{:S(2)}, u32[]{:S(2)}) collective-permute-start(f32[2,128,256]{2,1,0:T(8,128)S(1)} %get-tuple-element.96), channel_id=1, source_target_pairs={{1,0},{2,1},{3,2},{4,3},{5,4},{6,5},{7,6},{9,8},{10,9},{11,10},{12... | collective-permute-start | bytes 786440 | tf_op jit(solution)/shard_map/ppermute | solution.py:359
  133.8 12.5 %collective-permute-start.32 = (f32[2,128,256]{2,1,0:T(8,128)S(1)}, f32[2,128,256]{2,1,0:T(8,128)S(1)}, u32[]{:S(2)}, u32[]{:S(2)}) collective-permute-start(f32[2,128,256]{2,1,0:T(8,128)S(1)} %get-tuple-element.89), channel_id=1, source_target_pairs={{0,1},{1,2},{2,3},{3,4},{4,5},{5,6},{6,7},{8,9},{9,10},{10,11},{11... | collective-permute-start | bytes 786440 | tf_op jit(solution)/shard_map/ppermute | solution.py:359
  164.1 12.7 %collective-permute-start.37 = (f32[8,16,256]{2,1,0:T(8,128)S(1)}, f32[8,16,256]{2,1,0:T(8,128)S(1)}, u32[]{:S(2)}, u32[]{:S(2)}) collective-permute-start(f32[8,16,256]{2,1,0:T(8,128)S(1)} %get-tuple-element.106), channel_id=1, source_target_pairs={{0,32},{8,40},{16,48},{24,56},{32,64},{40,72},{48,80},{56,88},{64,... | collective-permute-start | bytes 393224 | tf_op jit(solution)/shard_map/ppermute | solution.py:366
  164.2 12.6 %collective-permute-start.38 = (f32[8,16,256]{2,1,0:T(8,128)S(1)}, f32[8,16,256]{2,1,0:T(8,128)S(1)}, u32[]{:S(2)}, u32[]{:S(2)}) collective-permute-start(f32[8,16,256]{2,1,0:T(8,128)S(1)} %get-tuple-element.107), channel_id=1, source_target_pairs={{0,224},{8,232},{16,240},{24,248},{32,0},{40,8},{48,16},{56,24},{6... | collective-permute-start | bytes 393224 | tf_op jit(solution)/shard_map/ppermute | solution.py:366
  170.5 10.0 %collective-permute-start.43 = (f32[8,16,256]{2,1,0:T(8,128)S(1)}, f32[8,16,256]{2,1,0:T(8,128)S(1)}, u32[]{:S(2)}, u32[]{:S(2)}) collective-permute-start(f32[8,16,256]{2,1,0:T(8,128)S(1)} %get-tuple-element.112), channel_id=1, source_target_pairs={{0,32},{8,40},{16,48},{24,56},{32,64},{40,72},{48,80},{56,88},{64,... | collective-permute-start | bytes 393224 | tf_op jit(solution)/shard_map/ppermute | solution.py:366
  (55 other events, 486.0 us)

commit v2 on v1

v2 whole, which is shorter than its diff:
```python
import functools

import jax
import jax.numpy as jnp
from jax import lax
from jax.experimental import pallas as pl
from jax.experimental.pallas import tpu as pltpu
from jax.sharding import PartitionSpec as P


ROWS, LANES = 32, 128
VMEM = pl.BlockSpec(memory_space=pltpu.VMEM)
SMEM = pl.BlockSpec(memory_space=pltpu.SMEM)


def shape(*dims):
    return jax.ShapeDtypeStruct(dims, jnp.float32)


def call(body, outs, args, scalars=0, scratch=(), out_specs=None, work=1.0, away=0):
    specs = [SMEM] * scalars + [VMEM] * (len(args) - scalars - away)
    specs += [pl.BlockSpec(memory_space=pltpu.HBM)] * away
    size = sum(4 * a.size for a in args) + sum(4 * o.size for o in outs)
    return pl.pallas_call(
        body,
        out_shape=tuple(outs),
        in_specs=specs,
        out_specs=tuple(out_specs or [VMEM] * len(outs)),
        scratch_shapes=list(scratch),
        compiler_params=pltpu.CompilerParams(vmem_limit_bytes=12 * 1024 * 1024),
        cost_estimate=pl.CostEstimate(
            flops=int(work * size * 4), bytes_accessed=size, transcendentals=0
        ),
    )(*args)


def edge_rows(load, start, count):
    parts = []
    low, high = max(start - 8, 0), min(start + ROWS + 8, count)
    body = load(low, high - low)
    blank = jnp.zeros((8, body.shape[1]), jnp.float32)
    if start == 0:
        parts.append(blank)
    parts.append(body)
    if start + ROWS == count:
        parts.append(blank)
    return jnp.concatenate(parts, axis=0) if len(parts) > 1 else body


def along_rows(wide, shift):
    return pltpu.roll(wide, shift % wide.shape[0], 0)[8 : 8 + ROWS]


def along_lanes(mid, lanes, shift):
    tiles = [mid[:, i : i + LANES] for i in range(0, mid.shape[1], LANES)]
    moved = [pltpu.roll(t, shift % LANES, 1) for t in tiles]
    out = []
    for i, own in enumerate(moved):
        j = i - 1 if shift > 0 else i + 1
        beside = moved[j] if 0 <= j < len(moved) else 0.0
        keep = lanes >= shift if shift > 0 else lanes < LANES + shift
        out.append(jnp.where(keep, own, beside))
    return jnp.concatenate(out, axis=1)


def lateral(wide, lanes):
    mid = wide[8 : 8 + ROWS]
    near = (along_rows(wide, 1) + along_rows(wide, -1)) + (
        along_lanes(mid, lanes, 1) + along_lanes(mid, lanes, -1)
    )
    far = (along_rows(wide, 2) + along_rows(wide, -2)) + (
        along_lanes(mid, lanes, 2) + along_lanes(mid, lanes, -2)
    )
    return 16.0 * near - far - 60.0 * mid


def vertical(ext, layer, rows):
    def at(offset):
        return ext[layer + offset, rows, :]

    return 16.0 * (at(1) + at(3)) - (at(0) + at(4)) - 30.0 * at(2)


def lane_index():
    return lax.broadcasted_iota(jnp.int32, (ROWS, LANES), 1)


def fill(ext, lo, hi):
    depth = ext.shape[0] - 4
    ext[0:2] = lo
    ext[depth + 2 : depth + 4] = hi


def put_ends(ref, lo_out, hi_out):
    depth = ref.shape[0]
    lo_out[...] = ref[0:2]
    hi_out[...] = ref[depth - 2 : depth]


def add_at(ref, cell, amount):
    _, width, length = ref.shape
    place = lax.broadcasted_iota(jnp.int32, (8, length), 0) * length
    place = place + lax.broadcasted_iota(jnp.int32, (8, length), 1)
    tile = cell // (8 * length)
    layer = tile // (width // 8)
    rows = pl.ds(pl.multiple_of((tile % (width // 8)) * 8, 8), 8)
    ref[layer, rows, :] = ref[layer, rows, :] + jnp.where(place == cell % (8 * length), amount, 0.0)


def forward_kernel(moment, *refs):
    it = iter(refs)
    info, pulse = next(it), next(it)
    state = next(it)
    if moment == 0:
        p_old, p_now, q_old, q_now = (state.at[0, i] for i in range(4))
    else:
        p_now, q_now = next(it), next(it)
        if moment == 1:
            p_old, q_old = state.at[0, 1], state.at[0, 3]
        else:
            p_old, q_old = state, next(it)
    stiff, stretch, lo, hi = (next(it) for _ in range(4))
    if moment == 2:
        back, side, one_in, two_in = (next(it) for _ in range(4))
    p_out, q_out = next(it), next(it)
    if moment < 2:
        lo_out, hi_out = next(it), next(it)
    first_out, second_out = next(it), next(it)
    ext = next(it)
    depth, width, _ = stiff.shape
    if moment == 0:
        fill(ext, lo[1], hi[1])
    else:
        fill(ext, lo[...], hi[...])
    lanes = lane_index()

    def copy(layer, _):
        ext[layer + 2] = q_now[layer]
        return 0

    lax.fori_loop(0, depth, copy, 0)

    def step(layer, _):
        for start in range(0, width, ROWS):
            rows = pl.ds(start, ROWS)
            flat = lateral(edge_rows(lambda s, n: p_now[layer, pl.ds(s, n), :], start, width), lanes)
            deep = vertical(ext, layer, rows)
            k = stiff[layer, rows, :]
            p_out[layer, rows, :] = (
                2.0 * p_now[layer, rows, :]
                - p_old[layer, rows, :]
                + k * (stretch[layer, rows, :] * flat + deep)
            )
            both = flat + deep
            q_out[layer, rows, :] = 2.0 * q_now[layer, rows, :] - q_old[layer, rows, :] + k * both
            if moment == 2:
                a, b = back[layer, rows, :], side[layer, rows, :]
                first_out[layer, rows, :] = one_in[layer, rows, :] + a * flat
                second_out[layer, rows, :] = two_in[layer, rows, :] + a * deep + b * both
            else:
                first_out[layer, rows, :] = flat
                second_out[layer, rows, :] = deep
        return 0

    lax.fori_loop(0, depth, step, 0)
    here = info[1] - info[0]

    @pl.when((here >= 0) & (here < info[3]))
    def _():
        add_at(p_out, here, pulse[0, moment])
        add_at(q_out, here, pulse[0, moment])

    if moment < 2:
        put_ends(q_out, lo_out, hi_out)


def last_kernel(p_now, q_now, back, side, one_in, two_in, lo, hi, one_out, two_out, lo_out, hi_out, ext):
    depth, width, length = p_now.shape
    zero = jnp.zeros((2, width, length), jnp.float32)
    fill(ext, zero, zero)
    lanes = lane_index()

    def copy(layer, _):
        ext[layer + 2] = q_now[layer]
        return 0

    lax.fori_loop(0, depth, copy, 0)

    def step(layer, _):
        for start in range(0, width, ROWS):
            rows = pl.ds(start, ROWS)
            flat = lateral(edge_rows(lambda s, n: p_now[layer, pl.ds(s, n), :], start, width), lanes)
            deep = vertical(ext, layer, rows)
            a, b = back[layer, rows, :], side[layer, rows, :]
            one_out[layer, rows, :] = one_in[layer, rows, :] + a * flat
            two_out[layer, rows, :] = two_in[layer, rows, :] + (a + b) * deep + b * flat
        return 0

    lax.fori_loop(0, depth, step, 0)
    lo_out[0] = -lo[0] * q_now[0]
    lo_out[1] = lo[1] * (16.0 * q_now[0] - q_now[1])
    hi_out[0] = hi[0] * (16.0 * q_now[depth - 1] - q_now[depth - 2])
    hi_out[1] = -hi[1] * q_now[depth - 1]


def adjoint_kernel(moment, *refs):
    it = iter(refs)
    _, count, cells, which, traces = (next(it) for _ in range(5))
    state = next(it)
    if moment == 3:
        a_old, a_now, b_old, b_now = (state.at[0, i] for i in range(4))
    else:
        a_now, b_now = next(it), next(it)
        if moment == 2:
            a_old, b_old = state.at[0, 1], state.at[0, 3]
        else:
            a_old, b_old = state, next(it)
    stiff, stretch = next(it), next(it)
    if moment > 1:
        lo, hi = next(it), next(it)
        a_out, b_out, lo_out, hi_out = (next(it) for _ in range(4))
    else:
        flat_in, deep_in = next(it), next(it)
        a_out, b_out, one_out, two_out = (next(it) for _ in range(4))
    ext = next(it)
    depth, width, length = stiff.shape
    if moment > 1:
        fill(ext, lo[...], hi[...])
    else:
        zero = jnp.zeros((2, width, length), jnp.float32)
        fill(ext, zero, zero)
    lanes = lane_index()

    def weigh(layer, _):
        ext[layer + 2] = stiff[layer] * (a_now[layer] + b_now[layer])
        return 0

    lax.fori_loop(0, depth, weigh, 0)

    def step(layer, _):
        for start in range(0, width, ROWS):
            rows = pl.ds(start, ROWS)

            def weighted(s, n):
                r = pl.ds(s, n)
                return stiff[layer, r, :] * (stretch[layer, r, :] * a_now[layer, r, :] + b_now[layer, r, :])

            flat = lateral(edge_rows(weighted, start, width), lanes)
            deep = vertical(ext, layer, rows)
            a_out[layer, rows, :] = 2.0 * a_now[layer, rows, :] - a_old[layer, rows, :] + flat
            b_out[layer, rows, :] = 2.0 * b_now[layer, rows, :] - b_old[layer, rows, :] + deep
        return 0

    lax.fori_loop(0, depth, step, 0)

    def drop(n, _):
        add_at(a_out, cells[n], traces[0, moment, which[n]])
        return 0

    lax.fori_loop(0, count[0], drop, 0)

    if moment > 1:
        for layer in range(2):
            lo_out[layer] = stiff[layer] * (a_out[layer] + b_out[layer])
            top = depth - 2 + layer
            hi_out[layer] = stiff[top] * (a_out[top] + b_out[top])
        return

    def image(layer, _):
        for start in range(0, width, ROWS):
            rows = pl.ds(start, ROWS)
            a, b = a_out[layer, rows, :], b_out[layer, rows, :]
            flat, deep = flat_in[layer, rows, :], deep_in[layer, rows, :]
            one_out[layer, rows, :] = a * flat
            two_out[layer, rows, :] = (a + b) * deep + b * flat
        return 0

    lax.fori_loop(0, depth, image, 0)


def final_kernel(*refs):
    info, count, cells, which, traces, pulse = refs[:6]
    a_now, b_part, a_old, b_old, stiff, stretch, lo, hi = refs[6:14]
    flat_two, deep_two, flat_in, deep_in, one_in, two_in = refs[14:20]
    lo_first, hi_first, lo_next, hi_next, lo_share, hi_share = refs[20:26]
    keep_out, send_out, ext, b_now, a_out, move = refs[26:]
    core = info[2]
    depth, width, length = stiff.shape
    zero = jnp.zeros((2, width, length), jnp.float32)
    fill(ext, zero, zero)
    lanes = lane_index()

    def fix(layer):
        if layer == 0:
            return 16.0 * lo[1] - lo[0]
        if layer == 1:
            return -lo[1]
        if layer == depth - 1:
            return 16.0 * hi[0] - hi[1]
        return -hi[0]

    ends = (0, 1, depth - 2, depth - 1)
    for n, layer in enumerate(ends):
        move[n] = fix(layer)
        b_now[layer] = b_part[layer] + move[n]

    def inner(layer, _):
        b_now[layer] = b_part[layer]
        return 0

    lax.fori_loop(2, depth - 2, inner, 0)

    def weigh(layer, _):
        ext[layer + 2] = stiff[layer] * (a_now[layer] + b_now[layer])
        return 0

    lax.fori_loop(0, depth, weigh, 0)

    def step(layer, _):
        for start in range(0, width, ROWS):
            rows = pl.ds(start, ROWS)

            def weighted(s, n):
                r = pl.ds(s, n)
                return stiff[layer, r, :] * (stretch[layer, r, :] * a_now[layer, r, :] + b_now[layer, r, :])

            flat = lateral(edge_rows(weighted, start, width), lanes)
            a_out[layer, rows, :] = 2.0 * a_now[layer, rows, :] - a_old[layer, rows, :] + flat
        return 0

    lax.fori_loop(0, depth, step, 0)

    def drop(n, _):
        add_at(a_out, cells[n], traces[0, 0, which[n]])
        return 0

    lax.fori_loop(0, count[0], drop, 0)

    def image(layer, _):
        for start in range(0, width, ROWS):
            rows = pl.ds(start, ROWS)
            a = a_out[layer, rows, :]
            b = 2.0 * b_now[layer, rows, :] - b_old[layer, rows, :] + vertical(ext, layer, rows)
            flat, deep = flat_in[layer, rows, :], deep_in[layer, rows, :]
            one = one_in[layer, rows, :] + a * flat
            two = two_in[layer, rows, :] + (a + b) * deep + b * flat

            @pl.when(core == 0)
            def _():
                keep_out[layer, rows, :] = one
                send_out[layer + 2, rows, :] = two

            @pl.when(core != 0)
            def _():
                send_out[layer, rows, :] = one
                keep_out[layer + 2, rows, :] = two

        return 0

    lax.fori_loop(0, depth, image, 0)
    gain = a_out
    gain[0:2] = lo_next[...] - 2.0 * lo_first[1] + lo_first[0]
    gain[2:4] = hi_next[...] - 2.0 * hi_first[1] + hi_first[0]
    plane = width * length
    here = info[1] - info[0]

    @pl.when((here >= -2 * plane) & (here < 0))
    def _():
        add_at(gain, here + 2 * plane, -pulse[0, 0])

    @pl.when((here >= depth * plane) & (here < (depth + 2) * plane))
    def _():
        add_at(gain, here - (depth - 2) * plane, -pulse[0, 0])

    def w(layer):
        return ext[layer + 2]

    low = (
        lo_share[0] - w(0) * gain[0],
        lo_share[1] + (16.0 * w(0) - w(1)) * gain[1],
    )
    high = (
        hi_share[0] + (16.0 * w(depth - 1) - w(depth - 2)) * gain[2],
        hi_share[1] - w(depth - 1) * gain[3],
    )
    change = [move[n] * (flat_two[l] + deep_two[l]) for n, l in enumerate(ends)]

    def finish(first, second):
        for n in range(2):
            first[depth + n] = low[n]
            second[n] = high[n]
        for n, l in enumerate(ends):
            second[l + 2] = second[l + 2] + change[n]

    @pl.when(core == 0)
    def _():
        finish(keep_out, send_out)

    @pl.when(core != 0)
    def _():
        finish(send_out, keep_out)


def receivers_kernel(info, receivers, count, cells, which):
    size = info[3]
    count[0] = 0

    def look(n, found):
        cell = receivers[0, n] - info[0]
        inside = (cell >= 0) & (cell < size)

        cells[found] = jnp.where(inside, cell, 0)
        which[found] = n
        return found + jnp.where(inside, 1, 0)

    count[0] = lax.fori_loop(0, receivers.shape[1], look, 0, unroll=8)


def quad_kernel(info, own, from_core, from_side, from_both, out):
    core, side = info[2], info[4]
    rows = own.shape[1]
    mine = own[...]
    for c in range(2):
        near = jnp.where(core == c, mine, from_core[...])
        far = jnp.where(core == c, from_side[...], from_both[...])
        out[:, rows * c : rows * (c + 1), :] = jnp.where(side == 0, near, far)
        out[:, rows * (2 + c) : rows * (3 + c), :] = jnp.where(side == 0, far, near)


def model_kernel(pieces, info, count, *refs):
    size = len(pieces)
    own, other = refs[:size], refs[size : 2 * size]
    low, high, stiff, stretch, lo_out, hi_out = refs[2 * size :]
    core, line = info[2], info[5]
    _, width, _ = stiff.shape
    band = own[0].shape[1]
    lines = width // band
    for mine, theirs, (steps, first) in zip(own, other, pieces):
        rows = pl.ds(pl.multiple_of(lax.rem(line + steps, lines) * band, band), band)
        for i in range(mine.shape[0]):
            layer = first + i - 2
            x, y = mine[i], theirs[i]
            vel = jnp.where(core == 0, x, y)
            rest = jnp.where(core == 0, y, x)
            k = vel * vel * (1.0 / 12.0)
            if layer < 0:
                lo_out[layer + 2, rows, :] = k * low[layer + 2, rows, :]
                above = rest * rest * (1.0 / 12.0)
                hi_out[layer + 2, rows, :] = above * high[layer + 2, rows, :]
            else:
                stiff[layer, rows, :] = k
                stretch[layer, rows, :] = 1.0 + 2.0 * rest


def split_kernel(info, keep, got, *outs):
    line = info[5]
    width = keep.shape[1]
    band = outs[0].shape[1]
    lines = width // band
    half = keep.shape[0] // 2
    for i, steps in enumerate((0, 1, 7, 2, 6, 3, 5)):
        rows = pl.ds(pl.multiple_of(lax.rem(line + steps, lines) * band, band), band)
        outs[i][...] = keep[:, rows, :] + got[:, rows, :]
    rows = pl.ds(pl.multiple_of(lax.rem(line + 4, lines) * band, band), band)
    outs[7][...] = keep[:half, rows, :] + got[:half, rows, :]
    outs[8][...] = keep[half:, rows, :] + got[half:, rows, :]


def relay_kernel(plus, minus, from_minus, from_plus, low, high, plus_out, minus_out):
    half = low.shape[0]
    plus_out[...] = plus[...] + from_minus[...]
    minus_out[...] = minus[...] + from_plus[...]
    plus_out[0:half] = plus_out[0:half] + low[...]
    minus_out[half:] = minus_out[half:] + high[...]


def lines_kernel(info, own, r1, r2, r3, r4, keep, send, straight, across):
    core, side = info[2], info[4]
    total = (own[...] + (r1[...] + r2[...])) + (r3[...] + r4[...])
    layers, rows, _ = keep.shape
    near = jnp.where(side == 0, total[:, :rows], total[:, rows:])
    far = jnp.where(side == 0, total[:, rows:], total[:, :rows])
    keep[...] = near
    send[...] = far
    straight[...] = jnp.where(core == 0, near[layers - 2 :], near[:2])
    across[...] = jnp.where(core == 0, far[layers - 2 :], far[:2])


def sides_kernel(info, keep, got, straight, across, mine, send):
    core = info[2]
    layers, width, _ = keep.shape
    rows = width // 2

    def place(first, count, total):
        low, high = total[:, :rows, :], total[:, rows:, :]
        mine[first : first + count] = jnp.where(core == 0, low, high)
        send[first : first + count] = jnp.where(core == 0, high, low)

    place(0, layers, keep[...] + got[...])
    place(layers, 2, straight[...] + across[...])


def gradient_kernel(info, mine, got, vel, eps, vel_out, eps_out):
    core = info[2]
    depth = vel.shape[0]
    one = jnp.where(core == 0, mine[:depth], got[:depth]) * (1.0 / 12.0)
    two = jnp.where(core == 0, got[2 : depth + 2], mine[2 : depth + 2]) * (1.0 / 12.0)
    from_above = jnp.where(core == 0, mine[depth + 2 :], got[depth + 2 :])
    from_below = jnp.where(core == 0, got[depth + 2 :], mine[depth + 2 :])
    v = vel[...]
    stiff = v * v
    vel_out[...] = 2.0 * v * ((1.0 + 2.0 * eps[...]) * one + two)
    for layer in range(2):
        top = depth - 2 + layer
        vel_out[layer] = vel_out[layer] + 2.0 * v[layer] * (from_below[layer] / stiff[layer])
        vel_out[top] = vel_out[top] + 2.0 * v[top] * (from_above[layer] / stiff[top])
    eps_out[...] = 2.0 * stiff * one


def on_device(
    velocity, epsilon, forward_state, adjoint_state, source_cell, wavelet, receiver_cells, residuals
):
    depth, share, length = velocity.shape
    width = forward_state.shape[3]
    shots = lax.axis_size("shot")
    slabs = lax.axis_size("dom")
    lines = shots // 4
    field = shape(depth, width, length)
    ends = shape(2, width, length)
    shot = lax.axis_index("shot")
    core, side, line = shot % 2, (shot // 2) % 2, shot // 4
    info = jnp.stack(
        [
            lax.axis_index("dom") * (depth * width * length),
            source_cell[0],
            core,
            jnp.int32(depth * width * length),
            side,
            line,
        ]
    ).astype(jnp.int32)

    up = [(i, i + 1) for i in range(slabs - 1)]
    down = [(i + 1, i) for i in range(slabs - 1)]

    def halos(lo, hi):
        return lax.ppermute(hi, "dom", up), lax.ppermute(lo, "dom", down)

    def swap(x, mask):
        return lax.ppermute(x, "shot", [(s, s ^ mask) for s in range(shots)])

    def from_line(x, steps):
        pairs = [(s, ((s // 4 - steps) % lines) * 4 + s % 4) for s in range(shots)]
        return lax.ppermute(x, "shot", pairs)

    below, above = halos(velocity[:2], velocity[depth - 2 :])
    first_part = jnp.concatenate([below, velocity], axis=0)
    second_part = jnp.concatenate([above, epsilon], axis=0)
    mine = jnp.where(core == 0, first_part, second_part)
    theirs = jnp.where(core == 0, second_part, first_part)
    from_side = swap(mine, 2)
    from_both = swap(theirs, 3)
    from_core = swap(theirs, 1)
    low_end, high_end = (
        jnp.concatenate(
            [forward_state[0, 2:4, rows], adjoint_state[0, 1:2, rows] + adjoint_state[0, 3:4, rows]], axis=0
        )
        for rows in (slice(0, 2), slice(depth - 2, depth))
    )
    q_lo, q_hi = halos(low_end, high_end)
    quad = call(
        quad_kernel,
        [shape(depth + 2, 4 * share, length)],
        (info, mine, from_core, from_side, from_both),
        1,
    )[0]
    half = depth // 2 + 1
    n2, m2 = from_line(quad, 2), from_line(quad, -2)
    n1, m1 = from_line(quad, 1), from_line(quad, -1)
    n3, m3 = from_line(n2, 1), from_line(m2, -1)
    low, high = from_line(n2[:half], 2), from_line(m2[half:], -2)
    blocks = (quad, n1, m1, n2, m2, n3, m3, low, high)
    pieces = ((0, 0), (1, 0), (7, 0), (2, 0), (6, 0), (3, 0), (5, 0), (4, 0), (4, half))
    other = tuple(swap(x, 1) for x in blocks)
    spots = jax.ShapeDtypeStruct((receiver_cells.shape[1] + 1,), jnp.int32)
    found = call(
        receivers_kernel,
        [jax.ShapeDtypeStruct((1,), jnp.int32), spots, spots],
        (info, receiver_cells),
        2,
        out_specs=[SMEM] * 3,
    )
    stiff, stretch, w_lo, w_hi = call(
        functools.partial(model_kernel, pieces),
        [field, field, ends, ends],
        (info, found[0], *blocks, *other, q_lo[2], q_hi[2]),
        2,
    )
    ext = pltpu.VMEM((depth + 4, width, length), jnp.float32)
    plane = pltpu.VMEM((depth, width, length), jnp.float32)
    model = (stiff, stretch)

    def forward(moment, outs, *args):
        body = functools.partial(forward_kernel, moment)
        return call(body, outs, (info, wavelet, *args), 2, [ext])

    def adjoint(moment, outs, *args):
        body = functools.partial(adjoint_kernel, moment)
        return call(body, outs, (info, *found, residuals, *args), 5, [ext])

    six = [field, field, ends, ends, field, field]
    p2, q2, lo, hi, flat1, deep1 = forward(0, six, forward_state, *model, q_lo, q_hi)
    q2_lo, q2_hi = halos(lo, hi)
    a4, b4, lo, hi = adjoint(3, six[:4], adjoint_state, *model, w_lo, w_hi)
    w3_lo, w3_hi = halos(lo, hi)
    p3, q3, lo, hi, flat2, deep2 = forward(1, six, forward_state, p2, q2, *model, q2_lo, q2_hi)
    q3_lo, q3_hi = halos(lo, hi)
    a3, b3, lo, hi = adjoint(2, six[:4], adjoint_state, a4, b4, *model, w3_lo, w3_hi)
    w2_lo, w2_hi = halos(lo, hi)
    a2, b2, one, two = adjoint(1, [field] * 4, a4, a3, b3, b4, *model, flat2, deep2)
    p4, q4, one, two = forward(2, [field] * 4, p2, p3, q3, q2, *model, q3_lo, q3_hi, a3, b3, one, two)
    one, two, lo_share, hi_share = call(
        last_kernel,
        [field, field, ends, ends],
        (p4, q4, a4, b4, one, two, w3_lo, w3_hi),
        0,
        [ext],
    )
    parts = shape(depth + 2, width, length)
    keep, send = call(
        final_kernel,
        [parts, parts],
        (info, *found, residuals, wavelet, a2, b2, a3, b3, *model, w2_lo, w2_hi)
        + (flat2, deep2, flat1, deep1, one, two, q_lo, q_hi, q2_lo, q2_hi, lo_share, hi_share),
        6,
        [ext, plane, plane, pltpu.VMEM((4, width, length), jnp.float32)],
    )

    band = shape(depth + 2, 4 * share, length)
    half_band = shape(half, 4 * share, length)
    got = swap(send, 1)
    own, s1, t1, s2, t2, s3, t3, low, high = call(
        split_kernel, [band] * 7 + [half_band] * 2, (info, keep, got), 1
    )
    g3, h3 = from_line(s3, -1), from_line(t3, 1)
    g4, h4 = from_line(low, -2), from_line(high, 2)
    s2, t2 = call(relay_kernel, [band] * 2, (s2, t2, g3, h3, g4, h4))
    got = [from_line(s2, -2), from_line(t2, 2), from_line(s1, -1), from_line(t1, 1)]

    def to_slab(x, mask):
        pairs = []
        for s in range(shots):
            for d in range(slabs):
                target = d - 1 if s % 2 == 0 else d + 1
                if 0 <= target < slabs:
                    pairs.append((s * slabs + d, (s ^ mask) * slabs + target))
        return lax.ppermute(x, ("shot", "dom"), pairs)

    pair, rest = shape(depth + 2, 2 * share, length), shape(2, 2 * share, length)
    keep, send, straight, across = call(lines_kernel, [pair, pair, rest, rest], (info, own, *got), 1)
    quarter = shape(depth + 4, share, length)
    keep, send = call(
        sides_kernel,
        [quarter, quarter],
        (info, keep, swap(send, 2), to_slab(straight, 0), to_slab(across, 2)),
        1,
    )
    vel_grad, eps_grad = call(
        gradient_kernel,
        [shape(depth, share, length)] * 2,
        (info, keep, swap(send, 1), velocity, epsilon),
        1,
    )
    return vel_grad, eps_grad


def solution(mesh):
    placed = (
        P("dom", "shot", None),
        P("dom", "shot", None),
        P("shot", None, "dom", None, None),
        P("shot", None, "dom", None, None),
        P("shot"),
        P("shot", None),
        P("shot", None),
        P("shot", None, None),
    )

    return jax.shard_map(
        on_device,
        mesh=mesh,
        in_specs=placed,
        out_specs=(P("dom", "shot", None), P("dom", "shot", None)),
        check_vma=False,
    )
```

time: 198 us -> 195 us (0.985)
  waiting for transfers between devices: 21.5 us -> 55.6 us
  local copies, waits for them, and re-layouts: 20.7 us -> 2.24 us
  Pallas kernels: 55.3 us -> 38 us
  starting transfers between devices: 96.4 us -> 94.3 us
    pallas_call x16, Pallas kernels: 55.3 us -> 38 us  [call(): pl.pallas_call(body, out_shape=tuple(outs), in_specs=specs, out_specs=tup...]
    unnamed x64 -> x16, local copies, waits for them, and re-layouts: 14.6 us -> 0.04 us
    ppermute x16, waiting for transfers between devices: 10.5 us -> 23 us  [from_line(): return lax.ppermute(x, 'shot', pairs)]
    ppermute x15, waiting for transfers between devices: 9.02 us -> 20.7 us  [swap(): return lax.ppermute(x, 'shot', [(s, s ^ mask) for s in range(shots)])]
    ppermute x16 -> x12, waiting for transfers between devices: 2.03 us -> 11.1 us  [halos(): return (lax.ppermute(hi, 'dom', up), lax.ppermute(lo, 'dom', down))]
    ppermute x0 -> x2, starting transfers between devices: none -> 7.51 us  [to_slab(): return lax.ppermute(x, ('shot', 'dom'), pairs)]
    squeeze x2 -> x3, local copies, waits for them, and re-layouts: 6.02 us -> 1.34 us  [the longest x1 1.3 us: on_device(): forward_state[0, 2:4, rows]]
    ppermute x16, starting transfers between devices: 30.1 us -> 25.5 us  [from_line(): return lax.ppermute(x, 'shot', pairs)]
  transfers between devices with their start and end apart: 47 -> 45, of which waited for: 11 -> 21; matrix products, arithmetic and copies ran while one was open for 3% -> 1% of each run, Pallas kernels for 23% -> 13%
where the time goes in v2:
time: 195 us; the launch traced here: 193 us
  starting transfers between devices  94.3 us (48%)
  waiting for transfers between devices  55.6 us (29%)
  Pallas kernels  38 us (19%)
  local copies, waits for them, and re-layouts  2.24 us (1%)
    ppermute x12, starting transfers between devices, halos(): return (lax.ppermute(hi, 'dom', up), lax.ppermute(lo, 'dom', down))  44.8 us
    pallas_call x16, Pallas kernels, call(): pl.pallas_call(body, out_shape=tuple(outs), in_specs=specs, out_specs=tup...  38 us
    ppermute x16, starting transfers between devices, from_line(): return lax.ppermute(x, 'shot', pairs)  25.5 us
    ppermute x16, waiting for transfers between devices, from_line(): return lax.ppermute(x, 'shot', pairs)  23 us
    ppermute x15, waiting for transfers between devices, swap(): return lax.ppermute(x, 'shot', [(s, s ^ mask) for s in range(shots)])  20.7 us
    ppermute x15, starting transfers between devices, swap(): return lax.ppermute(x, 'shot', [(s, s ^ mask) for s in range(shots)])  16.6 us
    ppermute x12, waiting for transfers between devices, halos(): return (lax.ppermute(hi, 'dom', up), lax.ppermute(lo, 'dom', down))  11.1 us
    ppermute x2, starting transfers between devices, to_slab(): return lax.ppermute(x, ('shot', 'dom'), pairs)  7.51 us
  transfers between devices with their start and end apart: 45, of which 21 were waited for; matrix products, arithmetic and copies ran while one was open for 1% of the time, Pallas kernels for 13%

profile of v2, /device:TPU:1, one launch (start us, length us, event | category | flops | bytes accessed | tf_op | source)
XLA Modules:
  0.0 193.4 jit_solution(4305724711618963690)
XLA Ops:
  2.7 4.6 %collective-permute-start = (f32[2,4,256]{2,1,0:T(4,128)S(1)}, f32[2,4,256]{2,1,0:T(4,128)S(1)}, u32[]{:S(2)}, u32[]{:S(2)}) collective-permute-start(f32[2,4,256]{2,1,0:T(4,128)S(1)} %get-tuple-element.125), channel_id=1, source_target_pairs={{0,1},{1,2},{2,3},{3,4},{4,5},{5,6},{6,7},{8,9},{9,10},{10,11},{11... | collective-permute-start | bytes 24584 | tf_op jit(solution)/shard_map/ppermute | solution.py:547
  9.9 4.3 %collective-permute-start.22 = (f32[3,2,128,256]{3,2,1,0:T(8,128)S(1)}, f32[3,2,128,256]{3,2,1,0:T(8,128)S(1)}, u32[]{:S(2)}, u32[]{:S(2)}) collective-permute-start(f32[3,2,128,256]{3,2,1,0:T(8,128)S(1)} %pad_maximum_fusion), channel_id=1, source_target_pairs={{0,1},{1,2},{2,3},{3,4},{4,5},{5,6},{6,7},{8,9},{9,10},{10,11},{11... | collective-permute-start | bytes 2359304 | tf_op jit(solution)/shard_map/ppermute | solution.py:547
  21.3 12.3 %collective-permute-done.3.from_side = f32[10,4,256]{2,1,0:T(4,128)S(1)} collective-permute-done((f32[10,4,256]{2,1,0:T(4,128)S(1)}, f32[10,4,256]{2,1,0:T(4,128)S(1)}, u32[]{:S(2)}, u32[]{:S(2)}) %collective-permute-start.3) | collective-permute-done | bytes 40992 | tf_op jit(solution)/shard_map/ppermute | solution.py:550
  36.7 5.7 %collective-permute-start.5 = (f32[10,16,256]{2,1,0:T(8,128)S(1)}, f32[10,16,256]{2,1,0:T(8,128)S(1)}, u32[]{:S(2)}, u32[]{:S(2)}) collective-permute-start(f32[10,16,256]{2,1,0:T(8,128)S(1)} %shard_map.96.refs_0_), channel_id=1, source_target_pairs={{0,224},{8,232},{16,240},{24,248},{32,0},{40,8},{48,16},{56,24},{6... | collective-permute-start | bytes 491528 | tf_op jit(solution)/shard_map/ppermute | solution.py:554
  44.8 3.5 %collective-permute-done.5.refs_1_ = f32[10,16,256]{2,1,0:T(8,128)S(1)} collective-permute-done((f32[10,16,256]{2,1,0:T(8,128)S(1)}, f32[10,16,256]{2,1,0:T(8,128)S(1)}, u32[]{:S(2)}, u32[]{:S(2)}) %collective-permute-start.5) | collective-permute-done | bytes 163872 | tf_op jit(solution)/shard_map/ppermute | solution.py:554
  48.3 4.4 %collective-permute-done.7.refs_3_ = f32[10,16,256]{2,1,0:T(8,128)S(1)} collective-permute-done((f32[10,16,256]{2,1,0:T(8,128)S(1)}, f32[10,16,256]{2,1,0:T(8,128)S(1)}, u32[]{:S(2)}, u32[]{:S(2)}) %collective-permute-start.7) | collective-permute-done | bytes 163872 | tf_op jit(solution)/shard_map/ppermute | solution.py:554
  54.7 3.7 %collective-permute-start.11 = (f32[5,16,256]{2,1,0:T(8,128)S(1)}, f32[5,16,256]{2,1,0:T(8,128)S(1)}, u32[]{:S(2)}, u32[]{:S(2)}) collective-permute-start(f32[5,16,256]{2,1,0:T(8,128)S(1)} %slice.48), channel_id=1, source_target_pairs={{0,192},{8,200},{16,208},{24,216},{32,224},{40,232},{48,240},{56,2... | collective-permute-start | bytes 245768 | tf_op jit(solution)/shard_map/ppermute | solution.py:554
  76.3 2.7 %shard_map.100 = (f32[8,128,256]{2,1,0:T(8,128)S(1)}, f32[8,128,256]{2,1,0:T(8,128)S(1)}, f32[2,128,256]{2,1,0:T(8,128)S(1)}, f32[2,128,256]{2,1,0:T(8,128)S(1)}...) custom-call(s32[6]{0:T(128)S(1)} %stack.19.info.refs_0_, f32[1,3]{1,0:T(1,128)S(1)} %copy-done.5, ...), custom_call_target="tpu_custom_call" | custom-call | flops 50331792 | bytes 12582948 | tf_op jit(solution)/shard_map/pallas_call | solution.py:24
  79.0 18.8 %collective-permute-start.26 = (f32[2,128,256]{2,1,0:T(8,128)S(1)}, f32[2,128,256]{2,1,0:T(8,128)S(1)}, u32[]{:S(2)}, u32[]{:S(2)}) collective-permute-start(f32[2,128,256]{2,1,0:T(8,128)S(1)} %get-tuple-element.75), channel_id=1, source_target_pairs={{0,1},{1,2},{2,3},{3,4},{4,5},{5,6},{6,7},{8,9},{9,10},{10,11},{11... | collective-permute-start | bytes 786440 | tf_op jit(solution)/shard_map/ppermute | solution.py:547
  99.2 4.6 %shard_map.98 = (f32[8,128,256]{2,1,0:T(8,128)S(1)}, f32[8,128,256]{2,1,0:T(8,128)S(1)}, f32[2,128,256]{2,1,0:T(8,128)S(1)}, f32[2,128,256]{2,1,0:T(8,128)S(1)}) custom-call(s32[6]{0:T(128)S(1)} %stack.19.info.refs_0_, s32[1]{0:T(128)} %get-tuple-element.60.count.refs_1_, s32[257]{0:T(512)S(1)} %get-tuple-element.61.refs_2_, ...), custom_call_target="tpu_custom_call" | custom-call | flops 37773456 | bytes 9443364 | tf_op jit(solution)/shard_map/pallas_call | solution.py:24
  103.8 4.7 %collective-permute-start.24 = (f32[2,128,256]{2,1,0:T(8,128)S(1)}, f32[2,128,256]{2,1,0:T(8,128)S(1)}, u32[]{:S(2)}, u32[]{:S(2)}) collective-permute-start(f32[2,128,256]{2,1,0:T(8,128)S(1)} %get-tuple-element.69), channel_id=1, source_target_pairs={{0,1},{1,2},{2,3},{3,4},{4,5},{5,6},{6,7},{8,9},{9,10},{10,11},{11... | collective-permute-start | bytes 786440 | tf_op jit(solution)/shard_map/ppermute | solution.py:547
  112.0 2.7 %shard_map.101 = (f32[8,128,256]{2,1,0:T(8,128)S(1)}, f32[8,128,256]{2,1,0:T(8,128)S(1)}, f32[2,128,256]{2,1,0:T(8,128)S(1)}, f32[2,128,256]{2,1,0:T(8,128)S(1)}...) custom-call(s32[6]{0:T(128)S(1)} %stack.19.info.refs_0_, f32[1,3]{1,0:T(1,128)S(1)} %copy-done.5, ...), custom_call_target="tpu_custom_call" | custom-call | flops 54526096 | bytes 13631524 | tf_op jit(solution)/shard_map/pallas_call | solution.py:24
  118.7 4.5 %collective-permute-done.25.refs_11_.hi = f32[2,128,256]{2,1,0:T(8,128)S(1)} collective-permute-done((f32[2,128,256]{2,1,0:T(8,128)S(1)}, f32[2,128,256]{2,1,0:T(8,128)S(1)}, u32[]{:S(2)}, u32[]{:S(2)}) %collective-permute-start.25) | collective-permute-done | bytes 262176 | tf_op jit(solution)/shard_map/ppermute | solution.py:547
  123.2 4.6 %shard_map.99 = (f32[8,128,256]{2,1,0:T(8,128)S(1)}, f32[8,128,256]{2,1,0:T(8,128)S(1)}, f32[2,128,256]{2,1,0:T(8,128)S(1)}, f32[2,128,256]{2,1,0:T(8,128)S(1)}) custom-call(s32[6]{0:T(128)S(1)} %stack.19.info.refs_0_, s32[1]{0:T(128)} %get-tuple-element.60.count.refs_1_, s32[257]{0:T(512)S(1)} %get-tuple-element.61.refs_2_, ...), custom_call_target="tpu_custom_call" | custom-call | flops 46162064 | bytes 11540516 | tf_op jit(solution)/shard_map/pallas_call | solution.py:24
  131.2 4.8 %shard_map.102 = (f32[8,128,256]{2,1,0:T(8,128)S(1)}, f32[8,128,256]{2,1,0:T(8,128)S(1)}, f32[8,128,256]{2,1,0:T(8,128)S(1)}, f32[8,128,256]{2,1,0:T(8,128)S(1)}) custom-call(s32[6]{0:T(128)S(1)} %stack.19.info.refs_0_, s32[1]{0:T(128)} %get-tuple-element.60.count.refs_1_, s32[257]{0:T(512)S(1)} %get-tuple-element.61.refs_2_, ...), custom_call_target="tpu_custom_call" | custom-call | flops 50356368 | bytes 12589092 | tf_op jit(solution)/shard_map/pallas_call | solution.py:24
  136.0 3.0 %shard_map.103 = (f32[8,128,256]{2,1,0:T(8,128)S(1)}, f32[8,128,256]{2,1,0:T(8,128)S(1)}, f32[8,128,256]{2,1,0:T(8,128)S(1)}, f32[8,128,256]{2,1,0:T(8,128)S(1)}) custom-call(s32[6]{0:T(128)S(1)} %stack.19.info.refs_0_, f32[1,3]{1,0:T(1,128)S(1)} %copy-done.5, f32[8,128,256]{2,1,0:T(8,128)S(1)} %get-tuple-element.73.refs_3_.refs_2_, ...), custom_call_target="tpu_custom_call" | custom-call | flops 60817552 | bytes 15204388 | tf_op jit(solution)/shard_map/pallas_call | solution.py:24
  141.3 4.4 %collective-permute-done.29.refs_13_ = f32[2,128,256]{2,1,0:T(8,128)S(1)} collective-permute-done((f32[2,128,256]{2,1,0:T(8,128)S(1)}, f32[2,128,256]{2,1,0:T(8,128)S(1)}, u32[]{:S(2)}, u32[]{:S(2)}) %collective-permute-start.29) | collective-permute-done | bytes 262176 | tf_op jit(solution)/shard_map/ppermute | solution.py:547
  145.7 5.8 %shard_map.105 = (f32[10,128,256]{2,1,0:T(8,128)S(1)}, f32[10,128,256]{2,1,0:T(8,128)S(1)}) custom-call(s32[6]{0:T(128)S(1)} %stack.19.info.refs_0_, s32[1]{0:T(128)} %get-tuple-element.60.count.refs_1_, s32[257]{0:T(512)S(1)} %get-tuple-element.61.refs_2_, s32[257]{0:T(512)S(1)} %get-tuple-element.62.refs_3_, f32[1,4,256]{2,1,0:T(4,128)S(1)} %copy-done.4, ...), custom_call_target="tpu_custom_call" | custom-call | flops 73425088 | bytes 18356272 | tf_op jit(solution)/shard_map/pallas_call | solution.py:24
  152.7 2.7 %collective-permute-done.32.got = f32[10,128,256]{2,1,0:T(8,128)S(1)} collective-permute-done((f32[10,128,256]{2,1,0:T(8,128)S(1)}, f32[10,128,256]{2,1,0:T(8,128)S(1)}, u32[]{:S(2)}, u32[]{:S(2)}) %collective-permute-start.32) | collective-permute-done | bytes 1310752 | tf_op jit(solution)/shard_map/ppermute | solution.py:550
  156.1 2.7 %collective-permute-start.34 = (f32[10,16,256]{2,1,0:T(8,128)S(1)}, f32[10,16,256]{2,1,0:T(8,128)S(1)}, u32[]{:S(2)}, u32[]{:S(2)}) collective-permute-start(f32[10,16,256]{2,1,0:T(8,128)S(1)} %get-tuple-element.105), channel_id=1, source_target_pairs={{0,224},{8,232},{16,240},{24,248},{32,0},{40,8},{48,16},{56,24},{6... | collective-permute-start | bytes 491528 | tf_op jit(solution)/shard_map/ppermute | solution.py:554
  158.8 3.6 %collective-permute-start.36 = (f32[5,16,256]{2,1,0:T(8,128)S(1)}, f32[5,16,256]{2,1,0:T(8,128)S(1)}, u32[]{:S(2)}, u32[]{:S(2)}) collective-permute-start(f32[5,16,256]{2,1,0:T(8,128)S(1)} %get-tuple-element.107), channel_id=1, source_target_pairs={{0,192},{8,200},{16,208},{24,216},{32,224},{40,232},{48,240},{56,2... | collective-permute-start | bytes 245768 | tf_op jit(solution)/shard_map/ppermute | solution.py:554
  170.3 5.6 %collective-permute-done.37.r1 = f32[10,16,256]{2,1,0:T(8,128)S(1)} collective-permute-done((f32[10,16,256]{2,1,0:T(8,128)S(1)}, f32[10,16,256]{2,1,0:T(8,128)S(1)}, u32[]{:S(2)}, u32[]{:S(2)}) %collective-permute-start.37) | collective-permute-done | bytes 163872 | tf_op jit(solution)/shard_map/ppermute | solution.py:554
  181.7 5.3 %collective-permute-start.43 = (f32[2,8,256]{2,1,0:T(8,128)S(1)}, f32[2,8,256]{2,1,0:T(8,128)S(1)}, u32[]{:S(2)}, u32[]{:S(2)}) collective-permute-start(f32[2,8,256]{2,1,0:T(8,128)S(1)} %get-tuple-element.115), channel_id=1, source_target_pairs={{1,16},{2,17},{3,18},{4,19},{5,20},{6,21},{7,22},{8,25},{9,26},{10... | collective-permute-start | bytes 49160 | tf_op jit(solution)/shard_map/ppermute | solution.py:657
  188.4 2.9 %collective-permute-start.44 = (f32[12,4,256]{2,1,0:T(4,128)S(1)}, f32[12,4,256]{2,1,0:T(4,128)S(1)}, u32[]{:S(2)}, u32[]{:S(2)}) collective-permute-start(f32[12,4,256]{2,1,0:T(4,128)S(1)} %get-tuple-element.117), channel_id=1, source_target_pairs={{0,8},{8,0},{16,24},{24,16},{32,40},{40,32},{48,56},{56,48},{64,72... | collective-permute-start | bytes 147464 | tf_op jit(solution)/shard_map/ppermute | solution.py:550
  (111 shorter events, 69.6 us)
Async XLA Ops:
  1.4 14.3 %collective-permute-start.1 = (f32[2,4,256]{2,1,0:T(4,128)S(1)}, f32[2,4,256]{2,1,0:T(4,128)S(1)}, u32[]{:S(2)}, u32[]{:S(2)}) collective-permute-start(f32[2,4,256]{2,1,0:T(4,128)S(1)} %get-tuple-element.124), channel_id=1, source_target_pairs={{1,0},{2,1},{3,2},{4,3},{5,4},{6,5},{7,6},{9,8},{10,9},{11,10},{12... | collective-permute-start | bytes 24584 | tf_op jit(solution)/shard_map/ppermute | solution.py:547
  2.7 12.9 %collective-permute-start = (f32[2,4,256]{2,1,0:T(4,128)S(1)}, f32[2,4,256]{2,1,0:T(4,128)S(1)}, u32[]{:S(2)}, u32[]{:S(2)}) collective-permute-start(f32[2,4,256]{2,1,0:T(4,128)S(1)} %get-tuple-element.125), channel_id=1, source_target_pairs={{0,1},{1,2},{2,3},{3,4},{4,5},{5,6},{6,7},{8,9},{9,10},{10,11},{11... | collective-permute-start | bytes 24584 | tf_op jit(solution)/shard_map/ppermute | solution.py:547
  9.9 56.5 %collective-permute-start.22 = (f32[3,2,128,256]{3,2,1,0:T(8,128)S(1)}, f32[3,2,128,256]{3,2,1,0:T(8,128)S(1)}, u32[]{:S(2)}, u32[]{:S(2)}) collective-permute-start(f32[3,2,128,256]{3,2,1,0:T(8,128)S(1)} %pad_maximum_fusion), channel_id=1, source_target_pairs={{0,1},{1,2},{2,3},{3,4},{4,5},{5,6},{6,7},{8,9},{9,10},{10,11},{11... | collective-permute-start | bytes 2359304 | tf_op jit(solution)/shard_map/ppermute | solution.py:547
  14.3 58.8 %collective-permute-start.23 = (f32[3,2,128,256]{3,2,1,0:T(8,128)S(1)}, f32[3,2,128,256]{3,2,1,0:T(8,128)S(1)}, u32[]{:S(2)}, u32[]{:S(2)}) collective-permute-start(f32[3,2,128,256]{3,2,1,0:T(8,128)S(1)} %pad_maximum_fusion.1), channel_id=1, source_target_pairs={{1,0},{2,1},{3,2},{4,3},{5,4},{6,5},{7,6},{9,8},{10,9},{11,10},{12... | collective-permute-start | bytes 2359304 | tf_op jit(solution)/shard_map/ppermute | solution.py:547
  17.3 16.3 %collective-permute-start.3 = (f32[10,4,256]{2,1,0:T(4,128)S(1)}, f32[10,4,256]{2,1,0:T(4,128)S(1)}, u32[]{:S(2)}, u32[]{:S(2)}) collective-permute-start(f32[10,4,256]{2,1,0:T(4,128)S(1)} %bitcast.20), channel_id=1, source_target_pairs={{0,16},{8,24},{16,0},{24,8},{32,48},{40,56},{48,32},{56,40},{64,80... | collective-permute-start | bytes 122888 | tf_op jit(solution)/shard_map/ppermute | solution.py:550
  19.8 16.4 %collective-permute-start.4 = (f32[10,4,256]{2,1,0:T(4,128)S(1)}, f32[10,4,256]{2,1,0:T(4,128)S(1)}, u32[]{:S(2)}, u32[]{:S(2)}) collective-permute-start(f32[10,4,256]{2,1,0:T(4,128)S(1)} %bitcast.25), channel_id=1, source_target_pairs={{0,24},{8,16},{16,8},{24,0},{32,56},{40,48},{48,40},{56,32},{64,88... | collective-permute-start | bytes 122888 | tf_op jit(solution)/shard_map/ppermute | solution.py:550
  36.7 11.6 %collective-permute-start.5 = (f32[10,16,256]{2,1,0:T(8,128)S(1)}, f32[10,16,256]{2,1,0:T(8,128)S(1)}, u32[]{:S(2)}, u32[]{:S(2)}) collective-permute-start(f32[10,16,256]{2,1,0:T(8,128)S(1)} %shard_map.96.refs_0_), channel_id=1, source_target_pairs={{0,224},{8,232},{16,240},{24,248},{32,0},{40,8},{48,16},{56,24},{6... | collective-permute-start | bytes 491528 | tf_op jit(solution)/shard_map/ppermute | solution.py:554
  42.4 10.3 %collective-permute-start.7 = (f32[10,16,256]{2,1,0:T(8,128)S(1)}, f32[10,16,256]{2,1,0:T(8,128)S(1)}, u32[]{:S(2)}, u32[]{:S(2)}) collective-permute-start(f32[10,16,256]{2,1,0:T(8,128)S(1)} %shard_map.96.refs_0_), channel_id=1, source_target_pairs={{0,192},{8,200},{16,208},{24,216},{32,224},{40,232},{48,240},{56,2... | collective-permute-start | bytes 491528 | tf_op jit(solution)/shard_map/ppermute | solution.py:554
  43.6 11.1 %collective-permute-start.8 = (f32[10,16,256]{2,1,0:T(8,128)S(1)}, f32[10,16,256]{2,1,0:T(8,128)S(1)}, u32[]{:S(2)}, u32[]{:S(2)}) collective-permute-start(f32[10,16,256]{2,1,0:T(8,128)S(1)} %shard_map.96.refs_0_), channel_id=1, source_target_pairs={{0,64},{8,72},{16,80},{24,88},{32,96},{40,104},{48,112},{56,120},{... | collective-permute-start | bytes 491528 | tf_op jit(solution)/shard_map/ppermute | solution.py:554
  48.3 10.0 %collective-permute-start.6 = (f32[10,16,256]{2,1,0:T(8,128)S(1)}, f32[10,16,256]{2,1,0:T(8,128)S(1)}, u32[]{:S(2)}, u32[]{:S(2)}) collective-permute-start(f32[10,16,256]{2,1,0:T(8,128)S(1)} %shard_map.96.refs_0_), channel_id=1, source_target_pairs={{0,32},{8,40},{16,48},{24,56},{32,64},{40,72},{48,80},{56,88},{64,... | collective-permute-start | bytes 491528 | tf_op jit(solution)/shard_map/ppermute | solution.py:554
  52.7 11.3 %collective-permute-start.13 = (f32[10,16,256]{2,1,0:T(8,128)S(1)}, f32[10,16,256]{2,1,0:T(8,128)S(1)}, u32[]{:S(2)}, u32[]{:S(2)}) collective-permute-start(f32[10,16,256]{2,1,0:T(8,128)S(1)} %shard_map.96.refs_0_), channel_id=1, source_target_pairs={{0,8},{8,0},{16,24},{24,16},{32,40},{40,32},{48,56},{56,48},{64,72... | collective-permute-start | bytes 491528 | tf_op jit(solution)/shard_map/ppermute | solution.py:550
  79.0 30.8 %collective-permute-start.26 = (f32[2,128,256]{2,1,0:T(8,128)S(1)}, f32[2,128,256]{2,1,0:T(8,128)S(1)}, u32[]{:S(2)}, u32[]{:S(2)}) collective-permute-start(f32[2,128,256]{2,1,0:T(8,128)S(1)} %get-tuple-element.75), channel_id=1, source_target_pairs={{0,1},{1,2},{2,3},{3,4},{4,5},{5,6},{6,7},{8,9},{9,10},{10,11},{11... | collective-permute-start | bytes 786440 | tf_op jit(solution)/shard_map/ppermute | solution.py:547
  97.9 14.1 %collective-permute-start.27 = (f32[2,128,256]{2,1,0:T(8,128)S(1)}, f32[2,128,256]{2,1,0:T(8,128)S(1)}, u32[]{:S(2)}, u32[]{:S(2)}) collective-permute-start(f32[2,128,256]{2,1,0:T(8,128)S(1)} %get-tuple-element.76), channel_id=1, source_target_pairs={{1,0},{2,1},{3,2},{4,3},{5,4},{6,5},{7,6},{9,8},{10,9},{11,10},{12... | collective-permute-start | bytes 786440 | tf_op jit(solution)/shard_map/ppermute | solution.py:547
  103.8 14.9 %collective-permute-start.24 = (f32[2,128,256]{2,1,0:T(8,128)S(1)}, f32[2,128,256]{2,1,0:T(8,128)S(1)}, u32[]{:S(2)}, u32[]{:S(2)}) collective-permute-start(f32[2,128,256]{2,1,0:T(8,128)S(1)} %get-tuple-element.69), channel_id=1, source_target_pairs={{0,1},{1,2},{2,3},{3,4},{4,5},{5,6},{6,7},{8,9},{9,10},{10,11},{11... | collective-permute-start | bytes 786440 | tf_op jit(solution)/shard_map/ppermute | solution.py:547
  108.5 14.7 %collective-permute-start.25 = (f32[2,128,256]{2,1,0:T(8,128)S(1)}, f32[2,128,256]{2,1,0:T(8,128)S(1)}, u32[]{:S(2)}, u32[]{:S(2)}) collective-permute-start(f32[2,128,256]{2,1,0:T(8,128)S(1)} %get-tuple-element.70), channel_id=1, source_target_pairs={{1,0},{2,1},{3,2},{4,3},{5,4},{6,5},{7,6},{9,8},{10,9},{11,10},{12... | collective-permute-start | bytes 786440 | tf_op jit(solution)/shard_map/ppermute | solution.py:547
  114.7 21.3 %collective-permute-start.30 = (f32[2,128,256]{2,1,0:T(8,128)S(1)}, f32[2,128,256]{2,1,0:T(8,128)S(1)}, u32[]{:S(2)}, u32[]{:S(2)}) collective-permute-start(f32[2,128,256]{2,1,0:T(8,128)S(1)} %get-tuple-element.87), channel_id=1, source_target_pairs={{0,1},{1,2},{2,3},{3,4},{4,5},{5,6},{6,7},{8,9},{9,10},{10,11},{11... | collective-permute-start | bytes 786440 | tf_op jit(solution)/shard_map/ppermute | solution.py:547
  117.4 18.6 %collective-permute-start.31 = (f32[2,128,256]{2,1,0:T(8,128)S(1)}, f32[2,128,256]{2,1,0:T(8,128)S(1)}, u32[]{:S(2)}, u32[]{:S(2)}) collective-permute-start(f32[2,128,256]{2,1,0:T(8,128)S(1)} %get-tuple-element.88), channel_id=1, source_target_pairs={{1,0},{2,1},{3,2},{4,3},{5,4},{6,5},{7,6},{9,8},{10,9},{11,10},{12... | collective-permute-start | bytes 786440 | tf_op jit(solution)/shard_map/ppermute | solution.py:547
  127.9 13.4 %collective-permute-start.28 = (f32[2,128,256]{2,1,0:T(8,128)S(1)}, f32[2,128,256]{2,1,0:T(8,128)S(1)}, u32[]{:S(2)}, u32[]{:S(2)}) collective-permute-start(f32[2,128,256]{2,1,0:T(8,128)S(1)} %get-tuple-element.81), channel_id=1, source_target_pairs={{0,1},{1,2},{2,3},{3,4},{4,5},{5,6},{6,7},{8,9},{9,10},{10,11},{11... | collective-permute-start | bytes 786440 | tf_op jit(solution)/shard_map/ppermute | solution.py:547
  129.9 15.8 %collective-permute-start.29 = (f32[2,128,256]{2,1,0:T(8,128)S(1)}, f32[2,128,256]{2,1,0:T(8,128)S(1)}, u32[]{:S(2)}, u32[]{:S(2)}) collective-permute-start(f32[2,128,256]{2,1,0:T(8,128)S(1)} %get-tuple-element.82), channel_id=1, source_target_pairs={{1,0},{2,1},{3,2},{4,3},{5,4},{6,5},{7,6},{9,8},{10,9},{11,10},{12... | collective-permute-start | bytes 786440 | tf_op jit(solution)/shard_map/ppermute | solution.py:547
  156.0 10.2 %collective-permute-start.33 = (f32[10,16,256]{2,1,0:T(8,128)S(1)}, f32[10,16,256]{2,1,0:T(8,128)S(1)}, u32[]{:S(2)}, u32[]{:S(2)}) collective-permute-start(f32[10,16,256]{2,1,0:T(8,128)S(1)} %get-tuple-element.104), channel_id=1, source_target_pairs={{0,32},{8,40},{16,48},{24,56},{32,64},{40,72},{48,80},{56,88},{64,... | collective-permute-start | bytes 491528 | tf_op jit(solution)/shard_map/ppermute | solution.py:554
  156.1 10.1 %collective-permute-start.34 = (f32[10,16,256]{2,1,0:T(8,128)S(1)}, f32[10,16,256]{2,1,0:T(8,128)S(1)}, u32[]{:S(2)}, u32[]{:S(2)}) collective-permute-start(f32[10,16,256]{2,1,0:T(8,128)S(1)} %get-tuple-element.105), channel_id=1, source_target_pairs={{0,224},{8,232},{16,240},{24,248},{32,0},{40,8},{48,16},{56,24},{6... | collective-permute-start | bytes 491528 | tf_op jit(solution)/shard_map/ppermute | solution.py:554
  166.3 9.6 %collective-permute-start.37 = (f32[10,16,256]{2,1,0:T(8,128)S(1)}, f32[10,16,256]{2,1,0:T(8,128)S(1)}, u32[]{:S(2)}, u32[]{:S(2)}) collective-permute-start(f32[10,16,256]{2,1,0:T(8,128)S(1)} %get-tuple-element.108), channel_id=1, source_target_pairs={{0,64},{8,72},{16,80},{24,88},{32,96},{40,104},{48,112},{56,120},{... | collective-permute-start | bytes 491528 | tf_op jit(solution)/shard_map/ppermute | solution.py:554
  168.3 10.1 %collective-permute-start.38 = (f32[10,16,256]{2,1,0:T(8,128)S(1)}, f32[10,16,256]{2,1,0:T(8,128)S(1)}, u32[]{:S(2)}, u32[]{:S(2)}) collective-permute-start(f32[10,16,256]{2,1,0:T(8,128)S(1)} %get-tuple-element.109), channel_id=1, source_target_pairs={{0,192},{8,200},{16,208},{24,216},{32,224},{40,232},{48,240},{56,2... | collective-permute-start | bytes 491528 | tf_op jit(solution)/shard_map/ppermute | solution.py:554
  179.0 8.9 %collective-permute-start.41 = (f32[10,8,256]{2,1,0:T(8,128)S(1)}, f32[10,8,256]{2,1,0:T(8,128)S(1)}, u32[]{:S(2)}, u32[]{:S(2)}) collective-permute-start(f32[10,8,256]{2,1,0:T(8,128)S(1)} %get-tuple-element.113), channel_id=1, source_target_pairs={{0,16},{8,24},{16,0},{24,8},{32,48},{40,56},{48,32},{56,40},{64,80... | collective-permute-start | bytes 245768 | tf_op jit(solution)/shard_map/ppermute | solution.py:550
  (28 other events, 367.2 us)

commit v3 on v2

--- a/solution.py
+++ b/solution.py
@@ -278,12 +278,35 @@
     lax.fori_loop(0, depth, image, 0)
 
 
+def adjoint_rows(layer, start, a_now, b_now, a_old, stiff, stretch, lanes):
+    def weighted(s, n):
+        r = pl.ds(s, n)
+        return stiff[layer, r, :] * (stretch[layer, r, :] * a_now[layer, r, :] + b_now[layer, r, :])
+
+    rows = pl.ds(start, ROWS)
+    flat = lateral(edge_rows(weighted, start, a_now.shape[1]), lanes)
+    return 2.0 * a_now[layer, rows, :] - a_old[layer, rows, :] + flat
+
+
+def inner_kernel(a_now, b_now, a_old, stiff, stretch, out):
+    depth, width, _ = stiff.shape
+    lanes = lane_index()
+
+    def step(layer, _):
+        for start in range(0, width, ROWS):
+            rows = pl.ds(start, ROWS)
+            out[layer - 2, rows, :] = adjoint_rows(layer, start, a_now, b_now, a_old, stiff, stretch, lanes)
+        return 0
+
+    lax.fori_loop(2, depth - 2, step, 0)
+
+
 def final_kernel(*refs):
     info, count, cells, which, traces, pulse = refs[:6]
     a_now, b_part, a_old, b_old, stiff, stretch, lo, hi = refs[6:14]
     flat_two, deep_two, flat_in, deep_in, one_in, two_in = refs[14:20]
-    lo_first, hi_first, lo_next, hi_next, lo_share, hi_share = refs[20:26]
-    keep_out, send_out, ext, b_now, a_out, move = refs[26:]
+    lo_first, hi_first, lo_next, hi_next, lo_share, hi_share, middle = refs[20:27]
+    keep_out, send_out, ext, b_now, a_out, move = refs[27:]
     core = info[2]
     depth, width, length = stiff.shape
     zero = jnp.zeros((2, width, length), jnp.float32)
@@ -306,6 +329,7 @@
 
     def inner(layer, _):
         b_now[layer] = b_part[layer]
+        a_out[layer] = middle[layer - 2]
         return 0
 
     lax.fori_loop(2, depth - 2, inner, 0)
@@ -316,19 +340,14 @@
 
     lax.fori_loop(0, depth, weigh, 0)
 
-    def step(layer, _):
+    def step(n, _):
+        layer = jnp.where(n < 2, n, n + depth - 4)
         for start in range(0, width, ROWS):
             rows = pl.ds(start, ROWS)
-
-            def weighted(s, n):
-                r = pl.ds(s, n)
-                return stiff[layer, r, :] * (stretch[layer, r, :] * a_now[layer, r, :] + b_now[layer, r, :])
-
-            flat = lateral(edge_rows(weighted, start, width), lanes)
-            a_out[layer, rows, :] = 2.0 * a_now[layer, rows, :] - a_old[layer, rows, :] + flat
-        return 0
-
-    lax.fori_loop(0, depth, step, 0)
+            a_out[layer, rows, :] = adjoint_rows(layer, start, a_now, b_now, a_old, stiff, stretch, lanes)
+        return 0
+
+    lax.fori_loop(0, 4, step, 0)
 
     def drop(n, _):
         add_at(a_out, cells[n], traces[0, 0, which[n]])
@@ -626,12 +645,13 @@
         0,
         [ext],
     )
+    middle = call(inner_kernel, [shape(depth - 4, width, length)], (a2, b2, a3, *model))[0]
     parts = shape(depth + 2, width, length)
     keep, send = call(
         final_kernel,
         [parts, parts],
         (info, *found, residuals, wavelet, a2, b2, a3, b3, *model, w2_lo, w2_hi)
-        + (flat2, deep2, flat1, deep1, one, two, q_lo, q_hi, q2_lo, q2_hi, lo_share, hi_share),
+        + (flat2, deep2, flat1, deep1, one, two, q_lo, q_hi, q2_lo, q2_hi, lo_share, hi_share, middle),
         6,
         [ext, plane, plane, pltpu.VMEM((4, width, length), jnp.float32)],
     )

time: 195 us -> 192 us (0.985)
  waiting for transfers between devices: 55.6 us -> 51.3 us
    ppermute x16, waiting for transfers between devices: 23 us -> 20 us  [from_line(): return lax.ppermute(x, 'shot', pairs)]
    ppermute x16, starting transfers between devices: 25.5 us -> 27.5 us  [from_line(): return lax.ppermute(x, 'shot', pairs)]
    pallas_call x16 -> x17, Pallas kernels: 38 us -> 38 us  [call(): pl.pallas_call(body, out_shape=tuple(outs), in_specs=specs, out_specs=tup...]
  transfers between devices with their start and end apart: 45 -> 45, of which waited for: 21 -> 18; matrix products, arithmetic and copies ran while one was open for 1% -> 1% of each run, Pallas kernels for 13% -> 14%
where the time goes in v3:
time: 192 us; the launch traced here: 190 us
  starting transfers between devices  95.6 us (50%)
  waiting for transfers between devices  51.3 us (27%)
  Pallas kernels  38 us (20%)
  local copies, waits for them, and re-layouts  2.24 us (1%)
    ppermute x12, starting transfers between devices, halos(): return (lax.ppermute(hi, 'dom', up), lax.ppermute(lo, 'dom', down))  44.8 us
    pallas_call x17, Pallas kernels, call(): pl.pallas_call(body, out_shape=tuple(outs), in_specs=specs, out_specs=tup...  38 us
    ppermute x16, starting transfers between devices, from_line(): return lax.ppermute(x, 'shot', pairs)  27.5 us
    ppermute x15, waiting for transfers between devices, swap(): return lax.ppermute(x, 'shot', [(s, s ^ mask) for s in range(shots)])  20.2 us
    ppermute x16, waiting for transfers between devices, from_line(): return lax.ppermute(x, 'shot', pairs)  20 us
    ppermute x15, starting transfers between devices, swap(): return lax.ppermute(x, 'shot', [(s, s ^ mask) for s in range(shots)])  15.3 us
    ppermute x12, waiting for transfers between devices, halos(): return (lax.ppermute(hi, 'dom', up), lax.ppermute(lo, 'dom', down))  10.2 us
    ppermute x2, starting transfers between devices, to_slab(): return lax.ppermute(x, ('shot', 'dom'), pairs)  7.97 us
  transfers between devices with their start and end apart: 45, of which 18 were waited for; matrix products, arithmetic and copies ran while one was open for 1% of the time, Pallas kernels for 14%

profile of v3, /device:TPU:1, one launch (start us, length us, event | category | flops | bytes accessed | tf_op | source)
XLA Modules:
  0.0 190.4 jit_solution(4049577645162817733)
XLA Ops:
  2.7 4.6 %collective-permute-start = (f32[2,4,256]{2,1,0:T(4,128)S(1)}, f32[2,4,256]{2,1,0:T(4,128)S(1)}, u32[]{:S(2)}, u32[]{:S(2)}) collective-permute-start(f32[2,4,256]{2,1,0:T(4,128)S(1)} %get-tuple-element.125), channel_id=1, source_target_pairs={{0,1},{1,2},{2,3},{3,4},{4,5},{5,6},{6,7},{8,9},{9,10},{10,11},{11... | collective-permute-start | bytes 24584 | tf_op jit(solution)/shard_map/ppermute | solution.py:566
  9.9 4.3 %collective-permute-start.22 = (f32[3,2,128,256]{3,2,1,0:T(8,128)S(1)}, f32[3,2,128,256]{3,2,1,0:T(8,128)S(1)}, u32[]{:S(2)}, u32[]{:S(2)}) collective-permute-start(f32[3,2,128,256]{3,2,1,0:T(8,128)S(1)} %pad_maximum_fusion), channel_id=1, source_target_pairs={{0,1},{1,2},{2,3},{3,4},{4,5},{5,6},{6,7},{8,9},{9,10},{10,11},{11... | collective-permute-start | bytes 2359304 | tf_op jit(solution)/shard_map/ppermute | solution.py:566
  21.0 14.7 %collective-permute-done.4.from_both = f32[10,4,256]{2,1,0:T(4,128)S(1)} collective-permute-done((f32[10,4,256]{2,1,0:T(4,128)S(1)}, f32[10,4,256]{2,1,0:T(4,128)S(1)}, u32[]{:S(2)}, u32[]{:S(2)}) %collective-permute-start.4) | collective-permute-done | bytes 40992 | tf_op jit(solution)/shard_map/ppermute | solution.py:569
  37.5 3.0 %collective-permute-start.8 = (f32[10,16,256]{2,1,0:T(8,128)S(1)}, f32[10,16,256]{2,1,0:T(8,128)S(1)}, u32[]{:S(2)}, u32[]{:S(2)}) collective-permute-start(f32[10,16,256]{2,1,0:T(8,128)S(1)} %shard_map.96.refs_0_), channel_id=1, source_target_pairs={{0,64},{8,72},{16,80},{24,88},{32,96},{40,104},{48,112},{56,120},{... | collective-permute-start | bytes 491528 | tf_op jit(solution)/shard_map/ppermute | solution.py:573
  40.5 3.0 %collective-permute-start.7 = (f32[10,16,256]{2,1,0:T(8,128)S(1)}, f32[10,16,256]{2,1,0:T(8,128)S(1)}, u32[]{:S(2)}, u32[]{:S(2)}) collective-permute-start(f32[10,16,256]{2,1,0:T(8,128)S(1)} %shard_map.96.refs_0_), channel_id=1, source_target_pairs={{0,192},{8,200},{16,208},{24,216},{32,224},{40,232},{48,240},{56,2... | collective-permute-start | bytes 491528 | tf_op jit(solution)/shard_map/ppermute | solution.py:573
  44.3 4.3 %collective-permute-done.8.refs_4_ = f32[10,16,256]{2,1,0:T(8,128)S(1)} collective-permute-done((f32[10,16,256]{2,1,0:T(8,128)S(1)}, f32[10,16,256]{2,1,0:T(8,128)S(1)}, u32[]{:S(2)}, u32[]{:S(2)}) %collective-permute-start.8) | collective-permute-done | bytes 163872 | tf_op jit(solution)/shard_map/ppermute | solution.py:573
  48.6 4.1 %collective-permute-start.5 = (f32[10,16,256]{2,1,0:T(8,128)S(1)}, f32[10,16,256]{2,1,0:T(8,128)S(1)}, u32[]{:S(2)}, u32[]{:S(2)}) collective-permute-start(f32[10,16,256]{2,1,0:T(8,128)S(1)} %shard_map.96.refs_0_), channel_id=1, source_target_pairs={{0,224},{8,232},{16,240},{24,248},{32,0},{40,8},{48,16},{56,24},{6... | collective-permute-start | bytes 491528 | tf_op jit(solution)/shard_map/ppermute | solution.py:573
  52.8 3.1 %collective-permute-start.12 = (f32[5,16,256]{2,1,0:T(8,128)S(1)}, f32[5,16,256]{2,1,0:T(8,128)S(1)}, u32[]{:S(2)}, u32[]{:S(2)}) collective-permute-start(f32[5,16,256]{2,1,0:T(8,128)S(1)} %slice.49), channel_id=1, source_target_pairs={{0,64},{8,72},{16,80},{24,88},{32,96},{40,104},{48,112},{56,120},{... | collective-permute-start | bytes 245768 | tf_op jit(solution)/shard_map/ppermute | solution.py:573
  58.9 2.8 %collective-permute-start.21 = (f32[5,16,256]{2,1,0:T(8,128)S(1)}, f32[5,16,256]{2,1,0:T(8,128)S(1)}, u32[]{:S(2)}, u32[]{:S(2)}) collective-permute-start(f32[5,16,256]{2,1,0:T(8,128)S(1)} %collective-permute-done.12.refs_8_), channel_id=1, source_target_pairs={{0,8},{8,0},{16,24},{24,16},{32,40},{40,32},{48,56},{56,48},{64,72... | collective-permute-start | bytes 245768 | tf_op jit(solution)/shard_map/ppermute | solution.py:569
  75.2 2.7 %shard_map.100 = (f32[8,128,256]{2,1,0:T(8,128)S(1)}, f32[8,128,256]{2,1,0:T(8,128)S(1)}, f32[2,128,256]{2,1,0:T(8,128)S(1)}, f32[2,128,256]{2,1,0:T(8,128)S(1)}...) custom-call(s32[6]{0:T(128)S(1)} %stack.19.info.refs_0_, f32[1,3]{1,0:T(1,128)S(1)} %copy-done.5, ...), custom_call_target="tpu_custom_call" | custom-call | flops 50331792 | bytes 12582948 | tf_op jit(solution)/shard_map/pallas_call | solution.py:24
  77.9 18.8 %collective-permute-start.26 = (f32[2,128,256]{2,1,0:T(8,128)S(1)}, f32[2,128,256]{2,1,0:T(8,128)S(1)}, u32[]{:S(2)}, u32[]{:S(2)}) collective-permute-start(f32[2,128,256]{2,1,0:T(8,128)S(1)} %get-tuple-element.75), channel_id=1, source_target_pairs={{0,1},{1,2},{2,3},{3,4},{4,5},{5,6},{6,7},{8,9},{9,10},{10,11},{11... | collective-permute-start | bytes 786440 | tf_op jit(solution)/shard_map/ppermute | solution.py:566
  98.1 4.6 %shard_map.98 = (f32[8,128,256]{2,1,0:T(8,128)S(1)}, f32[8,128,256]{2,1,0:T(8,128)S(1)}, f32[2,128,256]{2,1,0:T(8,128)S(1)}, f32[2,128,256]{2,1,0:T(8,128)S(1)}) custom-call(s32[6]{0:T(128)S(1)} %stack.19.info.refs_0_, s32[1]{0:T(128)} %get-tuple-element.60.count.refs_1_, s32[257]{0:T(512)S(1)} %get-tuple-element.61.refs_2_, ...), custom_call_target="tpu_custom_call" | custom-call | flops 37773456 | bytes 9443364 | tf_op jit(solution)/shard_map/pallas_call | solution.py:24
  102.7 4.7 %collective-permute-start.24 = (f32[2,128,256]{2,1,0:T(8,128)S(1)}, f32[2,128,256]{2,1,0:T(8,128)S(1)}, u32[]{:S(2)}, u32[]{:S(2)}) collective-permute-start(f32[2,128,256]{2,1,0:T(8,128)S(1)} %get-tuple-element.69), channel_id=1, source_target_pairs={{0,1},{1,2},{2,3},{3,4},{4,5},{5,6},{6,7},{8,9},{9,10},{10,11},{11... | collective-permute-start | bytes 786440 | tf_op jit(solution)/shard_map/ppermute | solution.py:566
  110.9 2.7 %shard_map.101 = (f32[8,128,256]{2,1,0:T(8,128)S(1)}, f32[8,128,256]{2,1,0:T(8,128)S(1)}, f32[2,128,256]{2,1,0:T(8,128)S(1)}, f32[2,128,256]{2,1,0:T(8,128)S(1)}...) custom-call(s32[6]{0:T(128)S(1)} %stack.19.info.refs_0_, f32[1,3]{1,0:T(1,128)S(1)} %copy-done.5, ...), custom_call_target="tpu_custom_call" | custom-call | flops 54526096 | bytes 13631524 | tf_op jit(solution)/shard_map/pallas_call | solution.py:24
  117.6 4.5 %collective-permute-done.25.refs_11_.hi = f32[2,128,256]{2,1,0:T(8,128)S(1)} collective-permute-done((f32[2,128,256]{2,1,0:T(8,128)S(1)}, f32[2,128,256]{2,1,0:T(8,128)S(1)}, u32[]{:S(2)}, u32[]{:S(2)}) %collective-permute-start.25) | collective-permute-done | bytes 262176 | tf_op jit(solution)/shard_map/ppermute | solution.py:566
  122.1 4.6 %shard_map.99 = (f32[8,128,256]{2,1,0:T(8,128)S(1)}, f32[8,128,256]{2,1,0:T(8,128)S(1)}, f32[2,128,256]{2,1,0:T(8,128)S(1)}, f32[2,128,256]{2,1,0:T(8,128)S(1)}) custom-call(s32[6]{0:T(128)S(1)} %stack.19.info.refs_0_, s32[1]{0:T(128)} %get-tuple-element.60.count.refs_1_, s32[257]{0:T(512)S(1)} %get-tuple-element.61.refs_2_, ...), custom_call_target="tpu_custom_call" | custom-call | flops 46162064 | bytes 11540516 | tf_op jit(solution)/shard_map/pallas_call | solution.py:24
  130.1 4.8 %shard_map.102 = (f32[8,128,256]{2,1,0:T(8,128)S(1)}, f32[8,128,256]{2,1,0:T(8,128)S(1)}, f32[8,128,256]{2,1,0:T(8,128)S(1)}, f32[8,128,256]{2,1,0:T(8,128)S(1)}) custom-call(s32[6]{0:T(128)S(1)} %stack.19.info.refs_0_, s32[1]{0:T(128)} %get-tuple-element.60.count.refs_1_, s32[257]{0:T(512)S(1)} %get-tuple-element.61.refs_2_, ...), custom_call_target="tpu_custom_call" | custom-call | flops 50356368 | bytes 12589092 | tf_op jit(solution)/shard_map/pallas_call | solution.py:24
  135.8 3.0 %shard_map.103 = (f32[8,128,256]{2,1,0:T(8,128)S(1)}, f32[8,128,256]{2,1,0:T(8,128)S(1)}, f32[8,128,256]{2,1,0:T(8,128)S(1)}, f32[8,128,256]{2,1,0:T(8,128)S(1)}) custom-call(s32[6]{0:T(128)S(1)} %stack.19.info.refs_0_, f32[1,3]{1,0:T(1,128)S(1)} %copy-done.5, f32[8,128,256]{2,1,0:T(8,128)S(1)} %get-tuple-element.73.refs_3_.refs_2_, ...), custom_call_target="tpu_custom_call" | custom-call | flops 60817552 | bytes 15204388 | tf_op jit(solution)/shard_map/pallas_call | solution.py:24
  141.1 3.5 %collective-permute-done.29.refs_13_ = f32[2,128,256]{2,1,0:T(8,128)S(1)} collective-permute-done((f32[2,128,256]{2,1,0:T(8,128)S(1)}, f32[2,128,256]{2,1,0:T(8,128)S(1)}, u32[]{:S(2)}, u32[]{:S(2)}) %collective-permute-start.29) | collective-permute-done | bytes 262176 | tf_op jit(solution)/shard_map/ppermute | solution.py:566
  144.6 4.9 %shard_map.106 = (f32[10,128,256]{2,1,0:T(8,128)S(1)}, f32[10,128,256]{2,1,0:T(8,128)S(1)}) custom-call(s32[6]{0:T(128)S(1)} %stack.19.info.refs_0_, s32[1]{0:T(128)} %get-tuple-element.60.count.refs_1_, s32[257]{0:T(512)S(1)} %get-tuple-element.61.refs_2_, s32[257]{0:T(512)S(1)} %get-tuple-element.62.refs_3_, f32[1,4,256]{2,1,0:T(4,128)S(1)} %copy-done.4, ...), custom_call_target="tpu_custom_call" | custom-call | flops 75522240 | bytes 18880560 | tf_op jit(solution)/shard_map/pallas_call | solution.py:24
  156.8 3.6 %collective-permute-start.36 = (f32[5,16,256]{2,1,0:T(8,128)S(1)}, f32[5,16,256]{2,1,0:T(8,128)S(1)}, u32[]{:S(2)}, u32[]{:S(2)}) collective-permute-start(f32[5,16,256]{2,1,0:T(8,128)S(1)} %get-tuple-element.107), channel_id=1, source_target_pairs={{0,192},{8,200},{16,208},{24,216},{32,224},{40,232},{48,240},{56,2... | collective-permute-start | bytes 245768 | tf_op jit(solution)/shard_map/ppermute | solution.py:573
  160.4 4.3 %collective-permute-done.35.low = f32[5,16,256]{2,1,0:T(8,128)S(1)} collective-permute-done((f32[5,16,256]{2,1,0:T(8,128)S(1)}, f32[5,16,256]{2,1,0:T(8,128)S(1)}, u32[]{:S(2)}, u32[]{:S(2)}) %collective-permute-start.35) | collective-permute-done | bytes 81952 | tf_op jit(solution)/shard_map/ppermute | solution.py:573
  168.9 6.2 %collective-permute-done.37.r1 = f32[10,16,256]{2,1,0:T(8,128)S(1)} collective-permute-done((f32[10,16,256]{2,1,0:T(8,128)S(1)}, f32[10,16,256]{2,1,0:T(8,128)S(1)}, u32[]{:S(2)}, u32[]{:S(2)}) %collective-permute-start.37) | collective-permute-done | bytes 163872 | tf_op jit(solution)/shard_map/ppermute | solution.py:573
  179.6 6.2 %collective-permute-start.43 = (f32[2,8,256]{2,1,0:T(8,128)S(1)}, f32[2,8,256]{2,1,0:T(8,128)S(1)}, u32[]{:S(2)}, u32[]{:S(2)}) collective-permute-start(f32[2,8,256]{2,1,0:T(8,128)S(1)} %get-tuple-element.115), channel_id=1, source_target_pairs={{1,16},{2,17},{3,18},{4,19},{5,20},{6,21},{7,22},{8,25},{9,26},{10... | collective-permute-start | bytes 49160 | tf_op jit(solution)/shard_map/ppermute | solution.py:677
  (112 shorter events, 65.1 us)
Async XLA Ops:
  1.4 14.3 %collective-permute-start.1 = (f32[2,4,256]{2,1,0:T(4,128)S(1)}, f32[2,4,256]{2,1,0:T(4,128)S(1)}, u32[]{:S(2)}, u32[]{:S(2)}) collective-permute-start(f32[2,4,256]{2,1,0:T(4,128)S(1)} %get-tuple-element.124), channel_id=1, source_target_pairs={{1,0},{2,1},{3,2},{4,3},{5,4},{6,5},{7,6},{9,8},{10,9},{11,10},{12... | collective-permute-start | bytes 24584 | tf_op jit(solution)/shard_map/ppermute | solution.py:566
  2.7 12.9 %collective-permute-start = (f32[2,4,256]{2,1,0:T(4,128)S(1)}, f32[2,4,256]{2,1,0:T(4,128)S(1)}, u32[]{:S(2)}, u32[]{:S(2)}) collective-permute-start(f32[2,4,256]{2,1,0:T(4,128)S(1)} %get-tuple-element.125), channel_id=1, source_target_pairs={{0,1},{1,2},{2,3},{3,4},{4,5},{5,6},{6,7},{8,9},{9,10},{10,11},{11... | collective-permute-start | bytes 24584 | tf_op jit(solution)/shard_map/ppermute | solution.py:566
  9.9 57.0 %collective-permute-start.22 = (f32[3,2,128,256]{3,2,1,0:T(8,128)S(1)}, f32[3,2,128,256]{3,2,1,0:T(8,128)S(1)}, u32[]{:S(2)}, u32[]{:S(2)}) collective-permute-start(f32[3,2,128,256]{3,2,1,0:T(8,128)S(1)} %pad_maximum_fusion), channel_id=1, source_target_pairs={{0,1},{1,2},{2,3},{3,4},{4,5},{5,6},{6,7},{8,9},{9,10},{10,11},{11... | collective-permute-start | bytes 2359304 | tf_op jit(solution)/shard_map/ppermute | solution.py:566
  14.3 57.8 %collective-permute-start.23 = (f32[3,2,128,256]{3,2,1,0:T(8,128)S(1)}, f32[3,2,128,256]{3,2,1,0:T(8,128)S(1)}, u32[]{:S(2)}, u32[]{:S(2)}) collective-permute-start(f32[3,2,128,256]{3,2,1,0:T(8,128)S(1)} %pad_maximum_fusion.1), channel_id=1, source_target_pairs={{1,0},{2,1},{3,2},{4,3},{5,4},{6,5},{7,6},{9,8},{10,9},{11,10},{12... | collective-permute-start | bytes 2359304 | tf_op jit(solution)/shard_map/ppermute | solution.py:566
  17.3 18.4 %collective-permute-start.4 = (f32[10,4,256]{2,1,0:T(4,128)S(1)}, f32[10,4,256]{2,1,0:T(4,128)S(1)}, u32[]{:S(2)}, u32[]{:S(2)}) collective-permute-start(f32[10,4,256]{2,1,0:T(4,128)S(1)} %bitcast.25), channel_id=1, source_target_pairs={{0,24},{8,16},{16,8},{24,0},{32,56},{40,48},{48,40},{56,32},{64,88... | collective-permute-start | bytes 122888 | tf_op jit(solution)/shard_map/ppermute | solution.py:569
  19.8 16.0 %collective-permute-start.3 = (f32[10,4,256]{2,1,0:T(4,128)S(1)}, f32[10,4,256]{2,1,0:T(4,128)S(1)}, u32[]{:S(2)}, u32[]{:S(2)}) collective-permute-start(f32[10,4,256]{2,1,0:T(4,128)S(1)} %bitcast.20), channel_id=1, source_target_pairs={{0,16},{8,24},{16,0},{24,8},{32,48},{40,56},{48,32},{56,40},{64,80... | collective-permute-start | bytes 122888 | tf_op jit(solution)/shard_map/ppermute | solution.py:569
  37.5 11.1 %collective-permute-start.8 = (f32[10,16,256]{2,1,0:T(8,128)S(1)}, f32[10,16,256]{2,1,0:T(8,128)S(1)}, u32[]{:S(2)}, u32[]{:S(2)}) collective-permute-start(f32[10,16,256]{2,1,0:T(8,128)S(1)} %shard_map.96.refs_0_), channel_id=1, source_target_pairs={{0,64},{8,72},{16,80},{24,88},{32,96},{40,104},{48,112},{56,120},{... | collective-permute-start | bytes 491528 | tf_op jit(solution)/shard_map/ppermute | solution.py:573
  40.5 12.2 %collective-permute-start.7 = (f32[10,16,256]{2,1,0:T(8,128)S(1)}, f32[10,16,256]{2,1,0:T(8,128)S(1)}, u32[]{:S(2)}, u32[]{:S(2)}) collective-permute-start(f32[10,16,256]{2,1,0:T(8,128)S(1)} %shard_map.96.refs_0_), channel_id=1, source_target_pairs={{0,192},{8,200},{16,208},{24,216},{32,224},{40,232},{48,240},{56,2... | collective-permute-start | bytes 491528 | tf_op jit(solution)/shard_map/ppermute | solution.py:573
  43.5 12.4 %collective-permute-start.6 = (f32[10,16,256]{2,1,0:T(8,128)S(1)}, f32[10,16,256]{2,1,0:T(8,128)S(1)}, u32[]{:S(2)}, u32[]{:S(2)}) collective-permute-start(f32[10,16,256]{2,1,0:T(8,128)S(1)} %shard_map.96.refs_0_), channel_id=1, source_target_pairs={{0,32},{8,40},{16,48},{24,56},{32,64},{40,72},{48,80},{56,88},{64,... | collective-permute-start | bytes 491528 | tf_op jit(solution)/shard_map/ppermute | solution.py:573
  48.6 15.4 %collective-permute-start.5 = (f32[10,16,256]{2,1,0:T(8,128)S(1)}, f32[10,16,256]{2,1,0:T(8,128)S(1)}, u32[]{:S(2)}, u32[]{:S(2)}) collective-permute-start(f32[10,16,256]{2,1,0:T(8,128)S(1)} %shard_map.96.refs_0_), channel_id=1, source_target_pairs={{0,224},{8,232},{16,240},{24,248},{32,0},{40,8},{48,16},{56,24},{6... | collective-permute-start | bytes 491528 | tf_op jit(solution)/shard_map/ppermute | solution.py:573
  55.9 8.2 %collective-permute-start.11 = (f32[5,16,256]{2,1,0:T(8,128)S(1)}, f32[5,16,256]{2,1,0:T(8,128)S(1)}, u32[]{:S(2)}, u32[]{:S(2)}) collective-permute-start(f32[5,16,256]{2,1,0:T(8,128)S(1)} %slice.48), channel_id=1, source_target_pairs={{0,192},{8,200},{16,208},{24,216},{32,224},{40,232},{48,240},{56,2... | collective-permute-start | bytes 245768 | tf_op jit(solution)/shard_map/ppermute | solution.py:573
  77.9 30.8 %collective-permute-start.26 = (f32[2,128,256]{2,1,0:T(8,128)S(1)}, f32[2,128,256]{2,1,0:T(8,128)S(1)}, u32[]{:S(2)}, u32[]{:S(2)}) collective-permute-start(f32[2,128,256]{2,1,0:T(8,128)S(1)} %get-tuple-element.75), channel_id=1, source_target_pairs={{0,1},{1,2},{2,3},{3,4},{4,5},{5,6},{6,7},{8,9},{9,10},{10,11},{11... | collective-permute-start | bytes 786440 | tf_op jit(solution)/shard_map/ppermute | solution.py:566
  96.8 14.1 %collective-permute-start.27 = (f32[2,128,256]{2,1,0:T(8,128)S(1)}, f32[2,128,256]{2,1,0:T(8,128)S(1)}, u32[]{:S(2)}, u32[]{:S(2)}) collective-permute-start(f32[2,128,256]{2,1,0:T(8,128)S(1)} %get-tuple-element.76), channel_id=1, source_target_pairs={{1,0},{2,1},{3,2},{4,3},{5,4},{6,5},{7,6},{9,8},{10,9},{11,10},{12... | collective-permute-start | bytes 786440 | tf_op jit(solution)/shard_map/ppermute | solution.py:566
  102.7 14.9 %collective-permute-start.24 = (f32[2,128,256]{2,1,0:T(8,128)S(1)}, f32[2,128,256]{2,1,0:T(8,128)S(1)}, u32[]{:S(2)}, u32[]{:S(2)}) collective-permute-start(f32[2,128,256]{2,1,0:T(8,128)S(1)} %get-tuple-element.69), channel_id=1, source_target_pairs={{0,1},{1,2},{2,3},{3,4},{4,5},{5,6},{6,7},{8,9},{9,10},{10,11},{11... | collective-permute-start | bytes 786440 | tf_op jit(solution)/shard_map/ppermute | solution.py:566
  107.4 14.7 %collective-permute-start.25 = (f32[2,128,256]{2,1,0:T(8,128)S(1)}, f32[2,128,256]{2,1,0:T(8,128)S(1)}, u32[]{:S(2)}, u32[]{:S(2)}) collective-permute-start(f32[2,128,256]{2,1,0:T(8,128)S(1)} %get-tuple-element.70), channel_id=1, source_target_pairs={{1,0},{2,1},{3,2},{4,3},{5,4},{6,5},{7,6},{9,8},{10,9},{11,10},{12... | collective-permute-start | bytes 786440 | tf_op jit(solution)/shard_map/ppermute | solution.py:566
  113.7 22.2 %collective-permute-start.30 = (f32[2,128,256]{2,1,0:T(8,128)S(1)}, f32[2,128,256]{2,1,0:T(8,128)S(1)}, u32[]{:S(2)}, u32[]{:S(2)}) collective-permute-start(f32[2,128,256]{2,1,0:T(8,128)S(1)} %get-tuple-element.87), channel_id=1, source_target_pairs={{0,1},{1,2},{2,3},{3,4},{4,5},{5,6},{6,7},{8,9},{9,10},{10,11},{11... | collective-permute-start | bytes 786440 | tf_op jit(solution)/shard_map/ppermute | solution.py:566
  116.3 19.5 %collective-permute-start.31 = (f32[2,128,256]{2,1,0:T(8,128)S(1)}, f32[2,128,256]{2,1,0:T(8,128)S(1)}, u32[]{:S(2)}, u32[]{:S(2)}) collective-permute-start(f32[2,128,256]{2,1,0:T(8,128)S(1)} %get-tuple-element.88), channel_id=1, source_target_pairs={{1,0},{2,1},{3,2},{4,3},{5,4},{6,5},{7,6},{9,8},{10,9},{11,10},{12... | collective-permute-start | bytes 786440 | tf_op jit(solution)/shard_map/ppermute | solution.py:566
  126.8 14.3 %collective-permute-start.28 = (f32[2,128,256]{2,1,0:T(8,128)S(1)}, f32[2,128,256]{2,1,0:T(8,128)S(1)}, u32[]{:S(2)}, u32[]{:S(2)}) collective-permute-start(f32[2,128,256]{2,1,0:T(8,128)S(1)} %get-tuple-element.81), channel_id=1, source_target_pairs={{0,1},{1,2},{2,3},{3,4},{4,5},{5,6},{6,7},{8,9},{9,10},{10,11},{11... | collective-permute-start | bytes 786440 | tf_op jit(solution)/shard_map/ppermute | solution.py:566
  128.8 15.8 %collective-permute-start.29 = (f32[2,128,256]{2,1,0:T(8,128)S(1)}, f32[2,128,256]{2,1,0:T(8,128)S(1)}, u32[]{:S(2)}, u32[]{:S(2)}) collective-permute-start(f32[2,128,256]{2,1,0:T(8,128)S(1)} %get-tuple-element.82), channel_id=1, source_target_pairs={{1,0},{2,1},{3,2},{4,3},{5,4},{6,5},{7,6},{9,8},{10,9},{11,10},{12... | collective-permute-start | bytes 786440 | tf_op jit(solution)/shard_map/ppermute | solution.py:566
  154.1 10.7 %collective-permute-start.33 = (f32[10,16,256]{2,1,0:T(8,128)S(1)}, f32[10,16,256]{2,1,0:T(8,128)S(1)}, u32[]{:S(2)}, u32[]{:S(2)}) collective-permute-start(f32[10,16,256]{2,1,0:T(8,128)S(1)} %get-tuple-element.104), channel_id=1, source_target_pairs={{0,32},{8,40},{16,48},{24,56},{32,64},{40,72},{48,80},{56,88},{64,... | collective-permute-start | bytes 491528 | tf_op jit(solution)/shard_map/ppermute | solution.py:573
  154.2 10.6 %collective-permute-start.34 = (f32[10,16,256]{2,1,0:T(8,128)S(1)}, f32[10,16,256]{2,1,0:T(8,128)S(1)}, u32[]{:S(2)}, u32[]{:S(2)}) collective-permute-start(f32[10,16,256]{2,1,0:T(8,128)S(1)} %get-tuple-element.105), channel_id=1, source_target_pairs={{0,224},{8,232},{16,240},{24,248},{32,0},{40,8},{48,16},{56,24},{6... | collective-permute-start | bytes 491528 | tf_op jit(solution)/shard_map/ppermute | solution.py:573
  164.8 10.3 %collective-permute-start.37 = (f32[10,16,256]{2,1,0:T(8,128)S(1)}, f32[10,16,256]{2,1,0:T(8,128)S(1)}, u32[]{:S(2)}, u32[]{:S(2)}) collective-permute-start(f32[10,16,256]{2,1,0:T(8,128)S(1)} %get-tuple-element.108), channel_id=1, source_target_pairs={{0,64},{8,72},{16,80},{24,88},{32,96},{40,104},{48,112},{56,120},{... | collective-permute-start | bytes 491528 | tf_op jit(solution)/shard_map/ppermute | solution.py:573
  167.2 9.0 %collective-permute-start.38 = (f32[10,16,256]{2,1,0:T(8,128)S(1)}, f32[10,16,256]{2,1,0:T(8,128)S(1)}, u32[]{:S(2)}, u32[]{:S(2)}) collective-permute-start(f32[10,16,256]{2,1,0:T(8,128)S(1)} %get-tuple-element.109), channel_id=1, source_target_pairs={{0,192},{8,200},{16,208},{24,216},{32,224},{40,232},{48,240},{56,2... | collective-permute-start | bytes 491528 | tf_op jit(solution)/shard_map/ppermute | solution.py:573
  176.7 10.0 %collective-permute-start.41 = (f32[10,8,256]{2,1,0:T(8,128)S(1)}, f32[10,8,256]{2,1,0:T(8,128)S(1)}, u32[]{:S(2)}, u32[]{:S(2)}) collective-permute-start(f32[10,8,256]{2,1,0:T(8,128)S(1)} %get-tuple-element.113), channel_id=1, source_target_pairs={{0,16},{8,24},{16,0},{24,8},{32,48},{40,56},{48,32},{56,40},{64,80... | collective-permute-start | bytes 245768 | tf_op jit(solution)/shard_map/ppermute | solution.py:569
  (28 other events, 363.3 us)
